TPU v7x, 32 devices: a whole 2x2x4 slice. The times are simulated.
32 devices in a mesh: band: 8 (over z, y), lev: 4 (over x, core).
Axes of the slice: x: 2, y: 2, z: 4, core: 2. Of those that a mesh axis runs over, the one named last changes fastest.
Arguments:
- winds: float32 [3, 4, 262144], P(None, 'lev', 'band'), may hold values from -6 to 6
- remap_w: float32 [4, 8, 4096], P(None, 'band'), may hold values from 0.1 to 1
- remap_col: int32 [4, 8, 4096], P(None, 'band'), may hold values from 0 to 1535
- block_pick: int32 [8, 96], replicated, may hold values from 0 to 255
- cycle_ids: int32 [8], P('band'), may hold values from 1024 to 3072
- wave_ids: int32 [2048], replicated, may hold values from 0 to 2047, each once
- legendre_a: bfloat16 [2048, 8, 2048], P(('band', 'lev')), may hold values from -0.03125 to 0.03125
- legendre_b: bfloat16 [2048, 8, 2048], P(('band', 'lev')), may hold values from -0.03125 to 0.03125
Outputs:
- divergence: float32 [2, 4, 2048, 2048], P(None, None, ('band', 'lev'))
- vorticity: float32 [2, 4, 2048, 2048], P(None, None, ('band', 'lev'))
Inputs may be any that keep to these rules, and one draw needn't show every extreme that they name: `block_pick`: block indices within one column shard. `remap_col`: offsets within the 12 picked blocks of one source column shard. `cycle_ids`: Equatorial-belt cycle numbers. `wave_ids`: each wavenumber below 2048 once.
All inputs are finite; a program needn't handle non-finite values.
Results may differ from a plain program's by a relative error of at most 0.0029.
Values may be sent and summed in bfloat16 or wider, within the bound.
No kernel may reach another device: no remote copies, remote signals or barrier semaphores. Data moves between devices by JAX's collectives and lax.ppermute only.
A program may use at most 192 MiB of HBM per device.

v0:
```python
import functools
import math

import jax
import jax.numpy as jnp
import numpy as np
from jax import lax
from jax.experimental import pallas as pl
from jax.experimental.pallas import tpu as pltpu
from jax.sharding import PartitionSpec as P

BLK = 128
LANES = 128
SUB = 8
HIGHEST = lax.Precision.HIGHEST


def pick_kernel(picks, winds, out, *, per):
    band = lax.axis_index("band")
    components = winds.shape[0]

    def one_target(t, carry):
        for c in range(per):
            block = picks[t, band * per + c]
            for comp in range(components):
                out[t, pl.ds(comp * per + c, 1), :] = winds[comp, pl.ds(block, 1), :]
        return carry

    lax.fori_loop(0, out.shape[0], one_target, 0, unroll=out.shape[0] <= 8)


def pick_blocks(block_pick, winds, band_count, per):
    components, blocks, _ = winds.shape
    return pl.pallas_call(
        functools.partial(pick_kernel, per=per),
        out_shape=jax.ShapeDtypeStruct((band_count, components * per, BLK), winds.dtype),
        in_specs=[
            pl.BlockSpec(memory_space=pltpu.SMEM),
            pl.BlockSpec(memory_space=pltpu.VMEM),
        ],
        out_specs=pl.BlockSpec(memory_space=pltpu.VMEM),
        name="pick",
    )(block_pick, winds)


@functools.lru_cache(maxsize=None)
def tables(cycle_length, taps, waves):
    rows = cycle_length // LANES
    b = np.arange(LANES, dtype=np.int64)
    lane_r = np.arange(taps * rows, dtype=np.int64) % rows
    p = np.arange(LANES, dtype=np.int64)
    u = np.arange(waves // LANES, dtype=np.int64)
    turn = 2.0 * np.pi
    azimuth = turn / cycle_length * (LANES * lane_r[None, :] + b[:, None] + 1)
    outer = turn / rows * (lane_r[:, None] * p[None, :] % rows)
    twist = turn / cycle_length * (b[:, None] * p[None, :] % cycle_length)
    inner = turn * ((LANES * u[:, None] * b[None, :]) % cycle_length) / cycle_length
    half_turn = turn / (2 * cycle_length) * (LANES * u[:, None] + p[None, :])
    f32 = np.float32
    return dict(
        azimuth=np.stack([np.cos(azimuth), np.sin(azimuth)]).astype(f32),
        outer=np.concatenate([np.cos(outer), -np.sin(outer)], 1).astype(f32),
        twist=np.stack([np.cos(twist), np.sin(twist)]).astype(f32),
        inner=np.block(
            [[np.cos(inner), np.sin(inner)], [-np.sin(inner), np.cos(inner)]]
        ).astype(f32),
        start=np.stack([np.cos(half_turn), np.sin(half_turn)]).astype(f32),
    )


def modes_kernel(
    cycle, received, col, weight, order, azimuth, outer, twist, inner, start, out, col_t, weight_t,
    cart, field, *, per, nside, paired
):
    band_count = received.shape[0]
    components = received.shape[1] // per
    tiles = LANES // SUB
    groups = band_count // SUB
    col_t[...] = jnp.transpose(col[...])
    weight_t[...] = jnp.transpose(weight[...])
    for comp in range(components):
        for group in range(groups):
            block_rows = [
                received[group * SUB : (group + 1) * SUB, comp * per + blk, :] for blk in range(per)
            ]
            for tile in range(group, tiles, groups):
                index = col_t[tile * SUB : (tile + 1) * SUB, :]
                lane = index & (BLK - 1)
                block = index >> (BLK.bit_length() - 1)
                value = jnp.take_along_axis(block_rows[0], lane, axis=1)
                for blk in range(1, per):
                    value = jnp.where(
                        block == blk, jnp.take_along_axis(block_rows[blk], lane, axis=1), value
                    )
                cart[comp, tile * SUB : (tile + 1) * SUB, :] = (
                    value * weight_t[tile * SUB : (tile + 1) * SUB, :]
                )
    number = cycle[0]
    half = lax.rem(number - nside + 1, 2) != 0
    spacing = math.pi / (2.0 * nside)
    turn_cos = jnp.where(half, math.cos(0.5 * spacing), 1.0).astype(jnp.float32)
    turn_sin = jnp.where(half, math.sin(0.5 * spacing), 0.0).astype(jnp.float32)
    number_f = jnp.full((SUB, LANES), number, jnp.int32).astype(jnp.float32)
    cos_tile = 4.0 / 3.0 - 2.0 * number_f / (3.0 * nside)
    sin_tile = jnp.sqrt(1.0 - cos_tile * cos_tile)
    cos_theta = cos_tile[:1, :]
    sin_theta = sin_tile[:1, :]
    cos_phi = azimuth[0] * turn_cos + azimuth[1] * turn_sin
    sin_phi = azimuth[1] * turn_cos - azimuth[0] * turn_sin
    x, y, z = cart[0], cart[1], cart[2]
    east = cos_phi * y - sin_phi * x
    north = sin_theta * z - cos_theta * (cos_phi * x + sin_phi * y)
    samples = jnp.concatenate([east, north], axis=0)
    section = jnp.dot(samples, outer[...], precision=HIGHEST, preferred_element_type=jnp.float32)
    turned_real = []
    turned_imag = []
    for f in range(2):
        real = section[f * LANES : (f + 1) * LANES, :LANES]
        imag = section[f * LANES : (f + 1) * LANES, LANES:]
        turned_real.append(real * twist[0] + imag * twist[1])
        turned_imag.append(imag * twist[0] - real * twist[1])
    turned = jnp.concatenate(
        [jnp.concatenate(turned_real, axis=1), jnp.concatenate(turned_imag, axis=1)], axis=0
    )
    spectrum = jnp.dot(inner[...], turned, precision=HIGHEST, preferred_element_type=jnp.float32)
    rows = start.shape[1]
    half_cos, half_sin = start[0], start[1]
    rot_cos = jnp.where(half, half_cos, half_cos * half_cos - half_sin * half_sin)
    rot_sin = jnp.where(half, half_sin, 2.0 * half_cos * half_sin)
    for f in range(2):
        real = spectrum[:rows, f * LANES : (f + 1) * LANES]
        imag = spectrum[rows:, f * LANES : (f + 1) * LANES]
        field[2 * f] = real * rot_cos + imag * rot_sin
        field[2 * f + 1] = imag * rot_cos - real * rot_sin
    low = lax.broadcasted_iota(jnp.int32, (SUB, LANES), 1) < LANES // 2
    for top in range(0, rows, SUB):
        wave = order[top : top + SUB, :]
        lane = wave & (LANES - 1)
        block = wave >> (LANES.bit_length() - 1)
        picked = []
        for k in range(4):
            value = None
            for blk in range(rows):
                source = jnp.broadcast_to(field[k, blk : blk + 1, :], (SUB, LANES))
                found = jnp.take_along_axis(source, lane, axis=1)
                value = found if value is None else jnp.where(block == blk, found, value)
            picked.append(value.astype(jnp.bfloat16).astype(jnp.float32))
        if paired:
            for h in range(2):
                first, second = picked[2 * h], picked[2 * h + 1]
                out[top : top + SUB, h, :] = jnp.where(
                    low, first, pltpu.roll(second, LANES // 2, axis=1)
                )
                out[top : top + SUB, 2 + h, :] = jnp.where(
                    low, pltpu.roll(first, LANES // 2, axis=1), second
                )
        else:
            for k in range(4):
                out[top : top + SUB, k, :] = picked[k]


def cycle_modes(cycle_ids, received, col, weight, order, taps, cycle_length, waves, per, paired):
    table = tables(cycle_length, taps, waves)
    names = ("azimuth", "outer", "twist", "inner", "start")
    components = received.shape[1] // per
    rows = waves // LANES
    vmem = pl.BlockSpec(memory_space=pltpu.VMEM)
    return pl.pallas_call(
        functools.partial(modes_kernel, per=per, nside=cycle_length // 4, paired=paired),
        out_shape=jax.ShapeDtypeStruct((rows, 4, LANES), jnp.float32),
        in_specs=[pl.BlockSpec(memory_space=pltpu.SMEM)] + [vmem] * 9,
        out_specs=vmem,
        scratch_shapes=[
            pltpu.VMEM((LANES, LANES), jnp.int32),
            pltpu.VMEM((LANES, LANES), jnp.float32),
            pltpu.VMEM((components, LANES, LANES), jnp.float32),
            pltpu.VMEM((4, rows, LANES), jnp.float32),
        ],
        name="modes",
    )(cycle_ids, received, col, weight, order, *[jnp.asarray(table[n]) for n in names])


PARTS = ((-1, 1, -1, 2), (1, 0, -1, 3), (-1, 3, 1, 0), (1, 2, 1, 1))


def legendre_kernel(modes, first_wave, table_a, table_b, div, vort, spread, *, levels, cycles, group, split):
    step = pl.program_id(0)
    owned = spread.shape[1]
    width = group * cycles

    @pl.when(step == 0)
    def _():
        rows = modes.shape[0]
        row = lax.broadcasted_iota(jnp.int32, (rows, levels * split * width), 0)
        lane = lax.broadcasted_iota(jnp.int32, (rows, levels * split * width), 1)
        same = (lax.rem(row, levels * split) == lax.div(lane, width)) & (
            lax.div(row, levels * split) == lax.rem(lane, cycles)
        )
        pick = jnp.where(same, 1.0, 0.0).astype(jnp.bfloat16)
        turned = jnp.transpose(modes[...]).astype(jnp.bfloat16)
        wide = jnp.dot(turned, pick, preferred_element_type=jnp.float32)
        slot = lax.broadcasted_iota(jnp.int32, (owned, width), 0)
        place = lax.broadcasted_iota(jnp.int32, (owned, width), 1)
        own = lax.rem(slot, group) == lax.div(place, cycles)
        for f in range(4):
            h, i = divmod(f, 4 // split)
            for lev in range(levels):
                start = (lev * split + h) * width
                part = wide[i * owned : (i + 1) * owned, start : start + width]
                spread[f * levels + lev] = jnp.where(own, part, 0.0).astype(jnp.bfloat16)

    base = pl.multiple_of(step * group, group)
    pieces = []
    for sign_a, field_a, sign_b, field_b in PARTS:
        for lev in range(levels):
            left = spread[field_a * levels + lev, pl.ds(base, group), :]
            right = spread[field_b * levels + lev, pl.ds(base, group), :]
            left = left if sign_a > 0 else -left
            right = right if sign_b > 0 else -right
            pieces.append(jnp.concatenate([left, right], axis=1))
    mix = jnp.concatenate(pieces, axis=0)
    degrees = table_a.shape[1]
    chunk = min(256, degrees)
    waves = first_wave[pl.ds(base, group), :]
    for start in range(0, degrees, chunk):
        both = jnp.concatenate(
            [table_a[:, start : start + chunk], table_b[:, start : start + chunk]], axis=0
        )
        result = jnp.dot(mix, both, preferred_element_type=jnp.float32)
        for at in range(0, chunk, LANES):
            degree = lax.broadcasted_iota(jnp.int32, (group, LANES), 1) + (start + at)
            upper = degree >= waves
            for part in range(4):
                target = div if part < 2 else vort
                for lev in range(levels):
                    top = (part * levels + lev) * group
                    target[part % 2, lev, :, start + at : start + at + LANES] = jnp.where(
                        upper, result[top : top + group, at : at + LANES], 0.0
                    )


def legendre_sums(modes, first_wave, legendre_a, legendre_b, levels, split):
    owned, cycles, degrees = legendre_a.shape
    group = math.gcd(owned, 16)
    flat = (owned * cycles, degrees)
    table_spec = pl.BlockSpec((group * cycles, degrees), lambda i: (i, 0))
    out_spec = pl.BlockSpec((2, levels, group, degrees), lambda i: (0, 0, i, 0))
    out_shape = jax.ShapeDtypeStruct((2, levels, owned, degrees), jnp.float32)
    return pl.pallas_call(
        functools.partial(
            legendre_kernel, levels=levels, cycles=cycles, group=group, split=split
        ),
        grid=(owned // group,),
        out_shape=(out_shape, out_shape),
        in_specs=[
            pl.BlockSpec(modes.shape, lambda i: (0, 0)),
            pl.BlockSpec(first_wave.shape, lambda i: (0, 0)),
            table_spec,
            table_spec,
        ],
        out_specs=(out_spec, out_spec),
        scratch_shapes=[pltpu.VMEM((4 * levels, owned, group * cycles), jnp.bfloat16)],
        name="legendre",
    )(modes, first_wave, legendre_a.reshape(flat), legendre_b.reshape(flat))


def local(winds, remap_w, remap_col, block_pick, cycle_ids, wave_ids, legendre_a, legendre_b):
    band_count = lax.axis_size("band")
    level_count = lax.axis_size("lev")
    components, levels_dev, column_count = winds.shape
    taps, cycle_count, cycle_length = remap_col.shape
    per = block_pick.shape[1] // band_count
    waves = wave_ids.shape[0]
    devices = band_count * level_count
    owned = waves // devices
    assert levels_dev == 1 and cycle_count == 1
    assert taps * cycle_length == LANES * LANES and band_count % SUB == 0
    blocks = winds.reshape(components, column_count // BLK, BLK)
    outgoing = pick_blocks(block_pick, blocks, band_count, per)
    received = lax.all_to_all(outgoing, "band", split_axis=0, concat_axis=0, tiled=True)
    paired = 2 * owned == LANES
    chosen = cycle_modes(
        cycle_ids,
        received,
        remap_col.reshape(LANES, LANES),
        remap_w.reshape(LANES, LANES),
        wave_ids.reshape(waves // LANES, LANES),
        taps,
        cycle_length,
        waves,
        per,
        paired,
    )
    split = 2 if paired else 1
    if paired:
        parcels = chosen.reshape(devices, split, LANES)
    else:
        parcels = jnp.transpose(
            jnp.transpose(chosen, (1, 0, 2)).reshape(4, devices, owned), (1, 0, 2)
        ).reshape(devices, 1, 4 * owned)
    gathered = lax.all_to_all(parcels, ("band", "lev"), split_axis=0, concat_axis=0, tiled=True)
    modes = gathered.reshape(devices * split, 4 * owned // split)
    slot_start = (lax.axis_index("band") * level_count + lax.axis_index("lev")) * owned
    my_waves = lax.dynamic_slice_in_dim(wave_ids, slot_start, owned)
    first_wave = jnp.broadcast_to(my_waves[:, None], (owned, LANES))
    return legendre_sums(modes, first_wave, legendre_a, legendre_b, level_count, split)


def solution(mesh):
    placed = (
        P(None, "lev", "band"),
        P(None, "band", None),
        P(None, "band", None),
        P(),
        P("band"),
        P(),
        P(("band", "lev"), None, None),
        P(("band", "lev"), None, None),
    )
    return jax.shard_map(
        local,
        mesh=mesh,
        in_specs=placed,
        out_specs=(P(None, None, ("band", "lev"), None), P(None, None, ("band", "lev"), None)),
        check_vma=False,
    )
```

profile of v0, /device:TPU:0, one launch (start us, length us, event | category | flops | bytes accessed | tf_op | source)
XLA Modules:
  0.0 39.4 jit_solution(11086881475573960174)
XLA Ops:
  0.6 1.8 %pick.1 = f32[8,36,128]{2,1,0:T(8,128)} custom-call(s32[8,96]{1,0:T(8,128)} %picks.1, f32[3,256,128]{2,1,0:T(8,128)} %bitcast.10), custom_call_target="tpu_custom_call" | custom-call | tf_op jit(solution)/shard_map/pick/pallas_call | solution.py:34
  2.5 7.3 %all-to-all-start = ((f32[8,36,128]{2,1,0:T(8,128)}), f32[8,36,128]{2,1,0:T(8,128)S(1)}, u32[]{:S(2)}, u32[]{:S(2)}) async-start(f32[8,36,128]{2,1,0:T(8,128)} %pick.1), calls=%async_computation | async-start | bytes 327680 | tf_op jit(solution)/shard_map/all_to_all | solution.py:280
  10.4 6.9 %all-to-all-done.received = f32[8,36,128]{2,1,0:T(8,128)S(1)} async-done(((f32[8,36,128]{2,1,0:T(8,128)}), f32[8,36,128]{2,1,0:T(8,128)S(1)}, u32[]{:S(2)}, u32[]{:S(2)}) %all-to-all-start) | async-done | bytes 147488 | tf_op jit(solution)/shard_map/all_to_all | solution.py:280
  17.3 0.0 copy-start
  17.3 0.7 %copy-done = f32[8,36,128]{2,1,0:T(8,128)} copy-done((f32[8,36,128]{2,1,0:T(8,128)}, f32[8,36,128]{2,1,0:T(8,128)S(1)}, u32[]{:S(2)}) %copy-start) | copy-done | bytes 147480
  18.0 3.8 %modes.1 = f32[16,4,128]{2,1,0:T(4,128)} custom-call(s32[1]{0:T(128)S(6)} %copy.15.cycle, f32[8,36,128]{2,1,0:T(8,128)} %copy-done, s32[128,128]{1,0:T(8,128)} %bitcast.13, f32[128,128]{1,0:T(8,128)} %bitcast.14, s32[16,128]{1,0:T(8,128)} %bitcast.15, f32[2,128,128]{2,1,0:T(8,128)} %constant.27.clone.azimuth, f32[128,256]{1,0:T(8,128)} %constant.28.clone.outer, ...), custom_call_target="tpu_custom_call" | custom-call | tf_op jit(solution)/shard_map/modes/pallas_call | solution.py:168
  21.8 2.8 %all-to-all-start.1 = ((f32[32,2,128]{2,1,0:T(2,128)}), f32[32,2,128]{2,1,0:T(2,128)S(1)}, u32[]{:S(2)}, u32[]{:S(2)}) async-start(f32[32,2,128]{2,1,0:T(2,128)} %bitcast.12), calls=%async_computation.1 | async-start | bytes 65536 | tf_op jit(solution)/shard_map/all_to_all | solution.py:301
  24.7 0.8 %dynamic_slice.3 = s32[64]{0:T(128)S(1)} dynamic-slice(s32[2048]{0:T(1024)} %param.18, s32[]{:T(128)S(6)} %select_n.3), dynamic_slice_sizes={64} | dynamic-slice | bytes 516 | tf_op jit(solution)/shard_map/dynamic_slice | solution.py:304
  25.5 6.5 %all-to-all-done.1 = f32[32,2,128]{2,1,0:T(2,128)S(1)} async-done(((f32[32,2,128]{2,1,0:T(2,128)}), f32[32,2,128]{2,1,0:T(2,128)S(1)}, u32[]{:S(2)}, u32[]{:S(2)}) %all-to-all-start.1) | async-done | bytes 32800 | tf_op jit(solution)/shard_map/all_to_all | solution.py:301
  32.0 0.0 copy-start.1
  32.0 0.7 %broadcast_in_dim.2.first_wave = s32[64,128]{1,0:T(8,128)} broadcast(s32[64]{0:T(128)S(1)} %dynamic_slice.3), dimensions={0} | broadcast | bytes 33024 | tf_op jit(solution)/shard_map/broadcast_in_dim | solution.py:305
  32.6 0.0 copy-done.1
  32.6 6.8 %legendre.1 = (f32[2,4,64,2048]{3,2,1,0:T(8,128)}, f32[2,4,64,2048]{3,2,1,0:T(8,128)}) custom-call(f32[64,128]{1,0:T(8,128)} %bitcast.11, s32[64,128]{1,0:T(8,128)} %broadcast_in_dim.2.first_wave, bf16[512,2048]{1,0:T(8,128)(2,1)} %bitcast.8, bf16[512,2048]{1,0:T(8,128)(2,1)} %bitcast.9), custom_call_target="tpu_custom_call" | custom-call | tf_op jit(solution)/shard_map/legendre/pallas_call | solution.py:249
Async XLA Ops:
  2.5 14.9 %all-to-all-start = ((f32[8,36,128]{2,1,0:T(8,128)}), f32[8,36,128]{2,1,0:T(8,128)S(1)}, u32[]{:S(2)}, u32[]{:S(2)}) async-start(f32[8,36,128]{2,1,0:T(8,128)} %pick.1), calls=%async_computation | async-start | bytes 327680 | tf_op jit(solution)/shard_map/all_to_all | solution.py:280
  17.3 0.7 %copy-start = (f32[8,36,128]{2,1,0:T(8,128)}, f32[8,36,128]{2,1,0:T(8,128)S(1)}, u32[]{:S(2)}) copy-start(f32[8,36,128]{2,1,0:T(8,128)S(1)} %all-to-all-done.received) | copy-start | bytes 442372
  21.8 10.1 %all-to-all-start.1 = ((f32[32,2,128]{2,1,0:T(2,128)}), f32[32,2,128]{2,1,0:T(2,128)S(1)}, u32[]{:S(2)}, u32[]{:S(2)}) async-start(f32[32,2,128]{2,1,0:T(2,128)} %bitcast.12), calls=%async_computation.1 | async-start | bytes 65536 | tf_op jit(solution)/shard_map/all_to_all | solution.py:301
  32.0 0.7 %copy-start.1 = (f32[32,2,128]{2,1,0:T(2,128)}, f32[32,2,128]{2,1,0:T(2,128)S(1)}, u32[]{:S(2)}) copy-start(f32[32,2,128]{2,1,0:T(2,128)S(1)} %all-to-all-done.1) | copy-start | bytes 98308
where the time goes:
time: 39.9 us; the launch traced here: 39.4 us
  waiting for transfers between devices  13.4 us (34%)
  Pallas kernels  12.5 us (31%)
  starting transfers between devices  10.2 us (26%)
  local copies, waits for them, and re-layouts  2.11 us (5%)
  between operations  1.3 us (3%)
    all_to_all x1, starting transfers between devices, local(): lax.all_to_all(outgoing, 'band', split_axis=0, concat_axis=0, tiled=True)  7.31 us
    all_to_all x1, waiting for transfers between devices, local(): lax.all_to_all(outgoing, 'band', split_axis=0, concat_axis=0, tiled=True)  6.91 us
    pallas_call x1, Pallas kernels, legendre_sums(): pl.pallas_call(functools.partial(legendre_kernel, levels=levels, cycles=c...  6.8 us
    all_to_all x1, waiting for transfers between devices, local(): lax.all_to_all(parcels, ('band', 'lev'), split_axis=0, concat_axis=0, til...  6.48 us
    pallas_call x1, Pallas kernels, cycle_modes(): pl.pallas_call(functools.partial(modes_kernel, per=per, nside=cycle_lengt...  3.83 us
    all_to_all x1, starting transfers between devices, local(): lax.all_to_all(parcels, ('band', 'lev'), split_axis=0, concat_axis=0, til...  2.85 us
    pallas_call x1, Pallas kernels, pick_blocks(): pl.pallas_call(functools.partial(pick_kernel, per=per), out_shape=jax.Sha...  1.84 us
  transfers between devices with their start and end apart: 2, of which 2 were waited for; matrix products, arithmetic and copies ran while one was open for 2% of the time, Pallas kernels for 0%

commit v1 on v0

v1 whole, which is shorter than its diff:
```python
import functools
import math

import jax
import jax.numpy as jnp
import numpy as np
from jax import lax
from jax.experimental import pallas as pl
from jax.experimental.pallas import tpu as pltpu
from jax.sharding import PartitionSpec as P

BLK = 128
LANES = 128
SUB = 8
VMEM_ALL = 67043328
ROOM = 12000 * 1024
HIGHEST = lax.Precision.HIGHEST


def pick_kernel(picks, winds, out, *, per):
    band = lax.axis_index("band")
    components = winds.shape[0]

    def one_target(t, carry):
        for c in range(per):
            block = picks[t, band * per + c]
            for comp in range(components):
                place, row = divmod(comp * per + c, out.shape[2])
                out[t, place, pl.ds(row, 1), :] = winds[comp, pl.ds(block, 1), :]
        return carry

    lax.fori_loop(0, out.shape[0], one_target, 0, unroll=out.shape[0] <= 8)


def pick_blocks(block_pick, winds, band_count, per):
    components, blocks, _ = winds.shape
    quad = math.gcd(components * per, 4)
    return pl.pallas_call(
        functools.partial(pick_kernel, per=per),
        out_shape=jax.ShapeDtypeStruct(
            (band_count, components * per // quad, quad, BLK), winds.dtype
        ),
        in_specs=[
            pl.BlockSpec(memory_space=pltpu.SMEM),
            pl.BlockSpec(memory_space=pltpu.VMEM),
        ],
        out_specs=pl.BlockSpec(memory_space=pltpu.VMEM),
        compiler_params=pltpu.CompilerParams(vmem_limit_bytes=VMEM_ALL),
        name="pick",
    )(block_pick, winds)


@functools.lru_cache(maxsize=None)
def tables(cycle_length, taps, waves):
    rows = cycle_length // LANES
    b = np.arange(LANES, dtype=np.int64)
    lane_r = np.arange(taps * rows, dtype=np.int64) % rows
    p = np.arange(LANES, dtype=np.int64)
    u = np.arange(waves // LANES, dtype=np.int64)
    turn = 2.0 * np.pi
    azimuth = turn / cycle_length * (LANES * lane_r[None, :] + b[:, None] + 1)
    outer = turn / rows * (lane_r[:, None] * p[None, :] % rows)
    twist = turn / cycle_length * (b[:, None] * p[None, :] % cycle_length)
    inner = turn * ((LANES * u[:, None] * b[None, :]) % cycle_length) / cycle_length
    half_turn = turn / (2 * cycle_length) * (LANES * u[:, None] + p[None, :])
    f32 = np.float32
    parts = dict(
        cos_phi=np.cos(azimuth),
        sin_phi=np.sin(azimuth),
        outer_real=np.cos(outer),
        outer_imag=-np.sin(outer),
        twist_cos=np.cos(twist),
        twist_sin=np.sin(twist),
        inner_real=np.concatenate([np.cos(inner), -np.sin(inner)], 0),
        inner_imag=np.concatenate([np.sin(inner), np.cos(inner)], 0),
        half_cos=np.cos(half_turn),
        half_sin=np.sin(half_turn),
    )
    spans = {}
    top = 0
    for name, part in parts.items():
        spans[name] = slice(top, top + part.shape[0])
        top += part.shape[0]
    spans["rest"] = slice(spans["outer_real"].start, top)
    return np.concatenate(list(parts.values()), 0).astype(np.float32), spans


def geometry_kernel(
    cycle, col, weight, order, table_hbm, col_t, weight_t, turn_cos, turn_sin, first_wave, rest,
    order_near, line, sems, *, spans, nside
):
    cos_phi = pltpu.make_async_copy(table_hbm.at[spans["cos_phi"], :], turn_cos, sems.at[0])
    sin_phi = pltpu.make_async_copy(table_hbm.at[spans["sin_phi"], :], turn_sin, sems.at[1])
    other = pltpu.make_async_copy(table_hbm.at[spans["rest"], :], rest, sems.at[2])
    cos_phi.start()
    sin_phi.start()
    other.start()
    col_t[...] = jnp.transpose(col[...])
    weight_t[...] = jnp.transpose(weight[...])
    order_near[...] = order[...]
    owned = first_wave.shape[0]
    slot = (lax.axis_index("band") * lax.axis_size("lev") + lax.axis_index("lev")) * owned
    mine = order[pl.ds(lax.div(slot, LANES), 1), :]
    line[...] = jnp.transpose(jnp.broadcast_to(mine, (LANES, LANES)))
    first_wave[...] = line[pl.ds(pl.multiple_of(lax.rem(slot, LANES), SUB), owned), :]
    half = lax.rem(cycle[0] - nside + 1, 2) != 0
    spacing = math.pi / (2.0 * nside)
    shift_cos = jnp.where(half, math.cos(0.5 * spacing), 1.0).astype(jnp.float32)
    shift_sin = jnp.where(half, math.sin(0.5 * spacing), 0.0).astype(jnp.float32)
    cos_phi.wait()
    sin_phi.wait()
    base_cos, base_sin = turn_cos[...], turn_sin[...]
    turn_cos[...] = base_cos * shift_cos + base_sin * shift_sin
    turn_sin[...] = base_sin * shift_cos - base_cos * shift_sin
    other.wait()


def cycle_geometry(cycle_ids, col, weight, order, owned, cycle_length, table, spans):
    vmem = pl.BlockSpec(memory_space=pltpu.VMEM)
    square = (LANES, LANES)
    rest = spans["rest"].stop - spans["rest"].start
    return pl.pallas_call(
        functools.partial(geometry_kernel, spans=spans, nside=cycle_length // 4),
        out_shape=(
            jax.ShapeDtypeStruct(square, jnp.int32),
            jax.ShapeDtypeStruct(square, jnp.float32),
            jax.ShapeDtypeStruct(square, jnp.float32),
            jax.ShapeDtypeStruct(square, jnp.float32),
            jax.ShapeDtypeStruct((owned, LANES), jnp.int32),
            jax.ShapeDtypeStruct((rest, LANES), jnp.float32),
            jax.ShapeDtypeStruct(order.shape, jnp.int32),
        ),
        in_specs=[pl.BlockSpec(memory_space=pltpu.SMEM), vmem, vmem, vmem]
        + [pl.BlockSpec(memory_space=pltpu.HBM)],
        out_specs=(vmem,) * 7,
        scratch_shapes=[pltpu.VMEM(square, jnp.int32), pltpu.SemaphoreType.DMA((3,))],
        compiler_params=pltpu.CompilerParams(vmem_limit_bytes=VMEM_ALL - ROOM),
        cost_estimate=pl.CostEstimate(flops=10**7, bytes_accessed=10**7, transcendentals=0),
        name="geometry",
    )(cycle_ids, col, weight, order, table)


def modes_kernel(
    cycle, received, col_t, weight_t, turn_cos, turn_sin, order, table, out, cart, field,
    *, spans, per, nside, paired
):
    band_count, _, quad, _ = received.shape
    components = cart.shape[0]
    tiles = LANES // SUB
    groups = band_count // SUB
    first = spans["rest"].start

    def part(name):
        return table[spans[name].start - first : spans[name].stop - first, :]

    for comp in range(components):
        for group in range(groups):
            block_rows = [
                received[(slice(group * SUB, (group + 1) * SUB), *divmod(comp * per + blk, quad))]
                for blk in range(per)
            ]
            for tile in range(group, tiles, groups):
                index = col_t[tile * SUB : (tile + 1) * SUB, :]
                lane = index & (BLK - 1)
                block = index >> (BLK.bit_length() - 1)
                value = jnp.take_along_axis(block_rows[0], lane, axis=1)
                for blk in range(1, per):
                    value = jnp.where(
                        block == blk, jnp.take_along_axis(block_rows[blk], lane, axis=1), value
                    )
                cart[comp, tile * SUB : (tile + 1) * SUB, :] = (
                    value * weight_t[tile * SUB : (tile + 1) * SUB, :]
                )
    number = cycle[0]
    half = lax.rem(number - nside + 1, 2) != 0
    number_f = jnp.full((SUB, LANES), number, jnp.int32).astype(jnp.float32)
    cos_tile = 4.0 / 3.0 - 2.0 * number_f / (3.0 * nside)
    sin_tile = jnp.sqrt(1.0 - cos_tile * cos_tile)
    cos_theta = cos_tile[:1, :]
    sin_theta = sin_tile[:1, :]
    cos_phi, sin_phi = turn_cos[...], turn_sin[...]
    x, y, z = cart[0], cart[1], cart[2]
    east = cos_phi * y - sin_phi * x
    north = sin_theta * z - cos_theta * (cos_phi * x + sin_phi * y)
    samples = jnp.concatenate([east, north], axis=0)
    outer = jnp.concatenate([part("outer_real"), part("outer_imag")], axis=1)
    section = jnp.dot(samples, outer, precision=HIGHEST, preferred_element_type=jnp.float32)
    twist_cos, twist_sin = part("twist_cos"), part("twist_sin")
    turned_real = []
    turned_imag = []
    for f in range(2):
        real = section[f * LANES : (f + 1) * LANES, :LANES]
        imag = section[f * LANES : (f + 1) * LANES, LANES:]
        turned_real.append(real * twist_cos + imag * twist_sin)
        turned_imag.append(imag * twist_cos - real * twist_sin)
    turned = jnp.concatenate(
        [jnp.concatenate(turned_real, axis=1), jnp.concatenate(turned_imag, axis=1)], axis=0
    )
    inner = jnp.concatenate([part("inner_real"), part("inner_imag")], axis=1)
    spectrum = jnp.dot(inner, turned, precision=HIGHEST, preferred_element_type=jnp.float32)
    rows = field.shape[1]
    half_cos, half_sin = part("half_cos"), part("half_sin")
    rot_cos = jnp.where(half, half_cos, half_cos * half_cos - half_sin * half_sin)
    rot_sin = jnp.where(half, half_sin, 2.0 * half_cos * half_sin)
    for f in range(2):
        real = spectrum[:rows, f * LANES : (f + 1) * LANES]
        imag = spectrum[rows:, f * LANES : (f + 1) * LANES]
        field[2 * f] = real * rot_cos + imag * rot_sin
        field[2 * f + 1] = imag * rot_cos - real * rot_sin
    low = lax.broadcasted_iota(jnp.int32, (SUB, LANES), 1) < LANES // 2
    for top in range(0, rows, SUB):
        wave = order[top : top + SUB, :]
        lane = wave & (LANES - 1)
        block = wave >> (LANES.bit_length() - 1)
        picked = []
        for k in range(4):
            value = None
            for blk in range(rows):
                source = jnp.broadcast_to(field[k, blk : blk + 1, :], (SUB, LANES))
                found = jnp.take_along_axis(source, lane, axis=1)
                value = found if value is None else jnp.where(block == blk, found, value)
            picked.append(value.astype(jnp.bfloat16).astype(jnp.float32))
        if paired:
            for h in range(2):
                first_f, second_f = picked[2 * h], picked[2 * h + 1]
                out[top : top + SUB, h, :] = jnp.where(
                    low, first_f, pltpu.roll(second_f, LANES // 2, axis=1)
                )
                out[top : top + SUB, 2 + h, :] = jnp.where(
                    low, pltpu.roll(first_f, LANES // 2, axis=1), second_f
                )
        else:
            for k in range(4):
                out[top : top + SUB, k, :] = picked[k]


def cycle_modes(cycle_ids, received, geometry, components, cycle_length, per, paired, spans):
    col_t, weight_t, turn_cos, turn_sin, _, rest, order = geometry
    rows = order.shape[0]
    vmem = pl.BlockSpec(memory_space=pltpu.VMEM)
    return pl.pallas_call(
        functools.partial(
            modes_kernel, spans=spans, per=per, nside=cycle_length // 4, paired=paired
        ),
        out_shape=jax.ShapeDtypeStruct((rows, 4, LANES), jnp.float32),
        in_specs=[pl.BlockSpec(memory_space=pltpu.SMEM)] + [vmem] * 7,
        out_specs=vmem,
        scratch_shapes=[
            pltpu.VMEM((components, LANES, LANES), jnp.float32),
            pltpu.VMEM((4, rows, LANES), jnp.float32),
        ],
        compiler_params=pltpu.CompilerParams(vmem_limit_bytes=VMEM_ALL - ROOM),
        name="modes",
    )(cycle_ids, received, col_t, weight_t, turn_cos, turn_sin, order, rest)


PARTS = ((-1, 1, -1, 2), (1, 0, -1, 3), (-1, 3, 1, 0), (1, 2, 1, 1))


def legendre_kernel(
    modes, first_wave, a_hbm, b_hbm, div_hbm, vort_hbm, table_a, table_b, spread, div, vort, in_sems,
    out_sems, *, levels, cycles, group, split
):
    owned = spread.shape[1]
    width = group * cycles
    groups = owned // group
    degrees = table_a.shape[1]

    def fetch(g, which):
        source, target = ((a_hbm, table_a), (b_hbm, table_b))[which]
        rows = pl.ds(g * width, width)
        return pltpu.make_async_copy(source.at[rows, :], target.at[rows, :], in_sems.at[g, which])

    def flush(g, which):
        source, target = ((div, div_hbm), (vort, vort_hbm))[which]
        rows = pl.ds(g * group, group)
        return pltpu.make_async_copy(
            source.at[:, :, rows, :], target.at[:, :, rows, :], out_sems.at[g, which]
        )

    for g in range(groups):
        for which in range(2):
            fetch(g, which).start()
    rows = modes.shape[0]
    row = lax.broadcasted_iota(jnp.int32, (rows, levels * split * width), 0)
    lane = lax.broadcasted_iota(jnp.int32, (rows, levels * split * width), 1)
    same = (lax.rem(row, levels * split) == lax.div(lane, width)) & (
        lax.div(row, levels * split) == lax.rem(lane, cycles)
    )
    pick = jnp.where(same, 1.0, 0.0).astype(jnp.bfloat16)
    turned = jnp.transpose(modes[...]).astype(jnp.bfloat16)
    wide = jnp.dot(turned, pick, preferred_element_type=jnp.float32)
    slot = lax.broadcasted_iota(jnp.int32, (owned, width), 0)
    place = lax.broadcasted_iota(jnp.int32, (owned, width), 1)
    own = lax.rem(slot, group) == lax.div(place, cycles)
    for f in range(4):
        h, i = divmod(f, 4 // split)
        for lev in range(levels):
            start = (lev * split + h) * width
            part = wide[i * owned : (i + 1) * owned, start : start + width]
            spread[f * levels + lev] = jnp.where(own, part, 0.0).astype(jnp.bfloat16)
    chunk = min(256, degrees)
    for g in range(groups):
        base = g * group
        pieces = []
        for sign_a, field_a, sign_b, field_b in PARTS:
            for lev in range(levels):
                left = spread[field_a * levels + lev, base : base + group, :]
                right = spread[field_b * levels + lev, base : base + group, :]
                left = left if sign_a > 0 else -left
                right = right if sign_b > 0 else -right
                pieces.append(jnp.concatenate([left, right], axis=1))
        mix = jnp.concatenate(pieces, axis=0)
        waves = first_wave[base : base + group, :]
        fetch(g, 0).wait()
        fetch(g, 1).wait()
        for start in range(0, degrees, chunk):
            at_rows = slice(g * width, (g + 1) * width)
            both = jnp.concatenate(
                [table_a[at_rows, start : start + chunk], table_b[at_rows, start : start + chunk]],
                axis=0,
            )
            result = jnp.dot(mix, both, preferred_element_type=jnp.float32)
            for at in range(0, chunk, LANES):
                degree = lax.broadcasted_iota(jnp.int32, (group, LANES), 1) + (start + at)
                upper = degree >= waves
                for part in range(4):
                    target = div if part < 2 else vort
                    for lev in range(levels):
                        top = (part * levels + lev) * group
                        lanes = slice(start + at, start + at + LANES)
                        target[part % 2, lev, base : base + group, lanes] = jnp.where(
                            upper, result[top : top + group, at : at + LANES], 0.0
                        )
        flush(g, 0).start()
        flush(g, 1).start()
    for g in range(groups):
        flush(g, 0).wait()
        flush(g, 1).wait()


def legendre_sums(modes, first_wave, legendre_a, legendre_b, levels, split):
    owned, cycles, degrees = legendre_a.shape
    group = math.gcd(owned, 16)
    flat = (owned * cycles, degrees)
    full = (2, levels, owned, degrees)
    out_shape = jax.ShapeDtypeStruct(full, jnp.float32)
    vmem = pl.BlockSpec(memory_space=pltpu.VMEM)
    hbm = pl.BlockSpec(memory_space=pltpu.HBM)
    return pl.pallas_call(
        functools.partial(
            legendre_kernel, levels=levels, cycles=cycles, group=group, split=split
        ),
        out_shape=(out_shape, out_shape),
        in_specs=[vmem, vmem, hbm, hbm],
        out_specs=(hbm, hbm),
        scratch_shapes=[
            pltpu.VMEM(flat, jnp.bfloat16),
            pltpu.VMEM(flat, jnp.bfloat16),
            pltpu.VMEM((4 * levels, owned, group * cycles), jnp.bfloat16),
            pltpu.VMEM(full, jnp.float32),
            pltpu.VMEM(full, jnp.float32),
            pltpu.SemaphoreType.DMA((owned // group, 2)),
            pltpu.SemaphoreType.DMA((owned // group, 2)),
        ],
        compiler_params=pltpu.CompilerParams(vmem_limit_bytes=VMEM_ALL - ROOM),
        name="legendre",
    )(modes, first_wave, legendre_a.reshape(flat), legendre_b.reshape(flat))


def local(winds, remap_w, remap_col, block_pick, cycle_ids, wave_ids, legendre_a, legendre_b):
    band_count = lax.axis_size("band")
    level_count = lax.axis_size("lev")
    components, levels_dev, column_count = winds.shape
    taps, cycle_count, cycle_length = remap_col.shape
    per = block_pick.shape[1] // band_count
    waves = wave_ids.shape[0]
    devices = band_count * level_count
    owned = waves // devices
    assert levels_dev == 1 and cycle_count == 1
    assert taps * cycle_length == LANES * LANES and band_count % SUB == 0
    blocks = winds.reshape(components, column_count // BLK, BLK)
    outgoing = pick_blocks(block_pick, blocks, band_count, per)
    received = lax.all_to_all(outgoing, "band", split_axis=0, concat_axis=0, tiled=True)
    paired = 2 * owned == LANES
    table, spans = tables(cycle_length, taps, waves)
    order = wave_ids.reshape(waves // LANES, LANES)
    geometry = cycle_geometry(
        cycle_ids,
        remap_col.reshape(LANES, LANES),
        remap_w.reshape(LANES, LANES),
        order,
        owned,
        cycle_length,
        jnp.asarray(table),
        spans,
    )
    chosen = cycle_modes(
        cycle_ids, received, geometry, components, cycle_length, per, paired, spans
    )
    first_wave = geometry[4]
    split = 2 if paired else 1
    if paired:
        parcels = chosen.reshape(devices, split, LANES)
    else:
        parcels = jnp.transpose(
            jnp.transpose(chosen, (1, 0, 2)).reshape(4, devices, owned), (1, 0, 2)
        ).reshape(devices, 1, 4 * owned)
    gathered = lax.all_to_all(parcels, ("band", "lev"), split_axis=0, concat_axis=0, tiled=True)
    modes = gathered.reshape(devices * split, 4 * owned // split)
    return legendre_sums(modes, first_wave, legendre_a, legendre_b, level_count, split)


def solution(mesh):
    placed = (
        P(None, "lev", "band"),
        P(None, "band", None),
        P(None, "band", None),
        P(),
        P("band"),
        P(),
        P(("band", "lev"), None, None),
        P(("band", "lev"), None, None),
    )
    return jax.shard_map(
        local,
        mesh=mesh,
        in_specs=placed,
        out_specs=(P(None, None, ("band", "lev"), None), P(None, None, ("band", "lev"), None)),
        check_vma=False,
    )
```

time: 39.9 us -> 34.7 us (0.87)
  waiting for transfers between devices: 13.4 us -> 3 us
  blocking collectives: 0 us -> 10.1 us
  Pallas kernels: 12.5 us -> 9.22 us
  starting transfers between devices: 10.2 us -> 7.31 us
  local copies, waits for them, and re-layouts: 2.11 us -> 3.38 us
    all_to_all x0 -> x1, blocking collectives: none -> 10.1 us  [local(): lax.all_to_all(parcels, ('band', 'lev'), split_axis=0, concat_axis=0, til...]
    all_to_all x1 -> x0, waiting for transfers between devices: 6.48 us -> none  [local(): lax.all_to_all(parcels, ('band', 'lev'), split_axis=0, concat_axis=0, til...]
    all_to_all x1, waiting for transfers between devices: 6.91 us -> 3 us  [local(): lax.all_to_all(outgoing, 'band', split_axis=0, concat_axis=0, tiled=True)]
    all_to_all x1 -> x0, starting transfers between devices: 2.85 us -> none  [local(): lax.all_to_all(parcels, ('band', 'lev'), split_axis=0, concat_axis=0, til...]
    unnamed x4 -> x8, local copies, waits for them, and re-layouts: 0.67 us -> 3.38 us
    pallas_call x1, Pallas kernels: 6.8 us -> 5.06 us  [legendre_sums(): pl.pallas_call(functools.partial(legendre_kernel, levels=levels, cycles=c...]
    pallas_call x1 -> x2, Pallas kernels: 3.83 us -> 2.33 us  [the longest x1 1.93 us: cycle_modes(): pl.pallas_call(functools.partial(modes_kernel, spans=spans, per=per, nsid...]
    dynamic_slice x1 -> x0, local copies, waits for them, and re-layouts: 0.76 us -> none  [local(): my_waves = lax.dynamic_slice_in_dim(wave_ids, slot_start, owned)]
  transfers between devices with their start and end apart: 2 -> 1, of which waited for: 2 -> 1; matrix products, arithmetic and copies ran while one was open for 2% -> 0% of each run, Pallas kernels for 0% -> 1%
where the time goes in v1:
time: 34.7 us; the launch traced here: 34.3 us
  blocking collectives  10.1 us (29%)
  Pallas kernels  9.22 us (27%)
  starting transfers between devices  7.31 us (21%)
  local copies, waits for them, and re-layouts  3.38 us (10%)
  waiting for transfers between devices  3 us (9%)
  between operations  1.31 us (4%)
    all_to_all x1, blocking collectives, local(): lax.all_to_all(parcels, ('band', 'lev'), split_axis=0, concat_axis=0, til...  10.1 us
    all_to_all x1, starting transfers between devices, local(): lax.all_to_all(outgoing, 'band', split_axis=0, concat_axis=0, tiled=True)  7.31 us
    pallas_call x1, Pallas kernels, legendre_sums(): pl.pallas_call(functools.partial(legendre_kernel, levels=levels, cycles=c...  5.06 us
    unnamed x8, local copies, waits for them, and re-layouts  3.38 us
    all_to_all x1, waiting for transfers between devices, local(): lax.all_to_all(outgoing, 'band', split_axis=0, concat_axis=0, tiled=True)  3 us
    pallas_call x1, Pallas kernels, cycle_modes(): pl.pallas_call(functools.partial(modes_kernel, spans=spans, per=per, nsid...  1.93 us
    pallas_call x1, Pallas kernels, pick_blocks(): pl.pallas_call(functools.partial(pick_kernel, per=per), out_shape=jax.Sha...  1.84 us
  transfers between devices with their start and end apart: 1, of which 1 were waited for; matrix products, arithmetic and copies ran while one was open for 0% of the time, Pallas kernels for 1%

profile of v1, /device:TPU:0, one launch (start us, length us, event | category | flops | bytes accessed | tf_op | source)
XLA Modules:
  0.0 34.3 jit_solution(5944021452747543628)
XLA Ops:
  0.6 1.8 %pick.1 = f32[8,9,4,128]{3,2,1,0:T(4,128)} custom-call(s32[8,96]{1,0:T(8,128)} %picks.1, f32[3,256,128]{2,1,0:T(8,128)} %bitcast.15), custom_call_target="tpu_custom_call" | custom-call | tf_op jit(solution)/shard_map/pick/pallas_call | solution.py:38
  2.5 7.3 %all-to-all-start = ((f32[8,9,4,128]{3,2,1,0:T(4,128)}), f32[8,9,4,128]{3,2,1,0:T(4,128)S(1)}, u32[]{:S(2)}, u32[]{:S(2)}) async-start(f32[8,9,4,128]{3,2,1,0:T(4,128)} %pick.1), calls=%async_computation | async-start | bytes 294912 | tf_op jit(solution)/shard_map/all_to_all | solution.py:384
  10.4 0.0 copy-start
  10.4 1.0 %copy-done = f32[864,128]{1,0:T(8,128)S(1)} copy-done((f32[864,128]{1,0:T(8,128)S(1)}, f32[864,128]{1,0:T(8,128)}, u32[]{:S(2)}) %copy-start) | copy-done | bytes 442392
  11.4 0.0 copy-start.1
  11.4 0.8 %copy-done.1 = s32[4,1,4096]{2,1,0:T(1,128)S(1)} copy-done((s32[4,1,4096]{2,1,0:T(1,128)S(1)}, s32[4,1,4096]{2,1,0:T(1,128)}, u32[]{:S(2)}) %copy-start.1) | copy-done | bytes 65560
  12.3 0.0 copy-start.2
  12.3 0.8 %copy-done.2 = f32[4,1,4096]{2,1,0:T(1,128)S(1)} copy-done((f32[4,1,4096]{2,1,0:T(1,128)S(1)}, f32[4,1,4096]{2,1,0:T(1,128)}, u32[]{:S(2)}) %copy-start.2) | copy-done | bytes 65560
  13.1 0.0 copy-start.3
  13.1 0.7 %copy-done.3 = s32[2048]{0:T(1024)S(1)} copy-done((s32[2048]{0:T(1024)S(1)}, s32[2048]{0:T(1024)}, u32[]{:S(2)}) %copy-start.3) | copy-done | bytes 8216
  13.8 0.4 %geometry.1 = (s32[128,128]{1,0:T(8,128)S(1)}, f32[128,128]{1,0:T(8,128)S(1)}, f32[128,128]{1,0:T(8,128)S(1)}, f32[128,128]{1,0:T(8,128)S(1)}, s32[64,128]{1,0:T...) custom-call(s32[1]{0:T(128)S(6)} %copy.11.cycle, s32[128,128]{1,0:T(8,128)S(1)} %bitcast.10, ...), custom_call_target="tpu_custom_call" | custom-call | flops 10000000 | bytes 10000000 | tf_op jit(solution)/shard_map/geometry/pallas_call | solution.py:122
  14.2 3.0 %all-to-all-done.received = f32[8,9,4,128]{3,2,1,0:T(4,128)S(1)} async-done(((f32[8,9,4,128]{3,2,1,0:T(4,128)}), f32[8,9,4,128]{3,2,1,0:T(4,128)S(1)}, u32[]{:S(2)}, u32[]{:S(2)}) %all-to-all-start) | async-done | bytes 147488 | tf_op jit(solution)/shard_map/all_to_all | solution.py:384
  17.2 1.9 %modes.1 = f32[16,4,128]{2,1,0:T(4,128)S(1)} custom-call(s32[1]{0:T(128)S(6)} %copy.11.cycle, f32[8,9,4,128]{3,2,1,0:T(4,128)S(1)} %all-to-all-done.received, s32[128,128]{1,0:T(8,128)S(1)} %get-tuple-element.9.col_t, f32[128,128]{1,0:T(8,128)S(1)} %get-tuple-element.10.weight_t, f32[128,128]{1,0:T(8,128)S(1)} %get-tuple-element.11.turn_cos, ...), custom_call_target="tpu_custom_call" | custom-call | tf_op jit(solution)/shard_map/modes/pallas_call | solution.py:241
  19.2 10.1 %all_to_all.10 = f32[32,2,128]{2,1,0:T(2,128)S(1)} all-to-all(f32[32,2,128]{2,1,0:T(2,128)S(1)} %bitcast.9), channel_id=1, replica_groups=mesh['band'=8,'lev'=4] {'band','lev'}, dimensions={0} | all-to-all | bytes 65536 | tf_op jit(solution)/shard_map/all_to_all | solution.py:409
  29.3 5.1 %legendre.1 = (f32[2,4,64,2048]{3,2,1,0:T(8,128)}, f32[2,4,64,2048]{3,2,1,0:T(8,128)}) custom-call(f32[64,128]{1,0:T(8,128)S(1)} %bitcast.8, s32[64,128]{1,0:T(8,128)S(1)} %get-tuple-element.15.first_wave, bf16[512,2048]{1,0:T(8,128)(2,1)} %bitcast.13, bf16[512,2048]{1,0:T(8,128)(2,1)} %bitcast.14), custom_call_target="tpu_custom_call" | custom-call | tf_op jit(solution)/shard_map/legendre/pallas_call | solution.py:350
Async XLA Ops:
  2.5 14.8 %all-to-all-start = ((f32[8,9,4,128]{3,2,1,0:T(4,128)}), f32[8,9,4,128]{3,2,1,0:T(4,128)S(1)}, u32[]{:S(2)}, u32[]{:S(2)}) async-start(f32[8,9,4,128]{3,2,1,0:T(4,128)} %pick.1), calls=%async_computation | async-start | bytes 294912 | tf_op jit(solution)/shard_map/all_to_all | solution.py:384
  10.4 1.0 %copy-start = (f32[864,128]{1,0:T(8,128)S(1)}, f32[864,128]{1,0:T(8,128)}, u32[]{:S(2)}) copy-start(f32[864,128]{1,0:T(8,128)} %constant.2.clone.table_hbm) | copy-start | bytes 1327108
  11.4 0.8 %copy-start.1 = (s32[4,1,4096]{2,1,0:T(1,128)S(1)}, s32[4,1,4096]{2,1,0:T(1,128)}, u32[]{:S(2)}) copy-start(s32[4,1,4096]{2,1,0:T(1,128)} %param.11) | copy-start | bytes 196612
  12.3 0.8 %copy-start.2 = (f32[4,1,4096]{2,1,0:T(1,128)S(1)}, f32[4,1,4096]{2,1,0:T(1,128)}, u32[]{:S(2)}) copy-start(f32[4,1,4096]{2,1,0:T(1,128)} %param.10) | copy-start | bytes 196612
  13.1 0.7 %copy-start.3 = (s32[2048]{0:T(1024)S(1)}, s32[2048]{0:T(1024)}, u32[]{:S(2)}) copy-start(s32[2048]{0:T(1024)} %param.14) | copy-start | bytes 24580

commit v2 on v1

--- a/solution.py
+++ b/solution.py
@@ -12,9 +12,15 @@
 BLK = 128
 LANES = 128
 SUB = 8
+GROUP = 16
+EARLY = 2
 VMEM_ALL = 67043328
-ROOM = 12000 * 1024
+ROOM = 24000 * 1024
 HIGHEST = lax.Precision.HIGHEST
+
+
+def far(array):
+    return pltpu.with_memory_space_constraint(array, pltpu.HBM)
 
 
 def pick_kernel(picks, winds, out, *, per):
@@ -45,9 +51,9 @@
             pl.BlockSpec(memory_space=pltpu.VMEM),
         ],
         out_specs=pl.BlockSpec(memory_space=pltpu.VMEM),
-        compiler_params=pltpu.CompilerParams(vmem_limit_bytes=VMEM_ALL),
+        compiler_params=pltpu.CompilerParams(vmem_limit_bytes=VMEM_ALL - ROOM),
         name="pick",
-    )(block_pick, winds)
+    )(far(block_pick), far(winds))
 
 
 @functools.lru_cache(maxsize=None)
@@ -85,16 +91,26 @@
     return np.concatenate(list(parts.values()), 0).astype(np.float32), spans
 
 
+def early_shape(flat, owned):
+    group = math.gcd(owned, GROUP)
+    return (2, min(EARLY, owned // group) * group * (flat[0] // owned), flat[1])
+
+
 def geometry_kernel(
-    cycle, col, weight, order, table_hbm, col_t, weight_t, turn_cos, turn_sin, first_wave, rest,
-    order_near, line, sems, *, spans, nside
+    cycle, col, weight, order, table_hbm, a_hbm, b_hbm, col_t, weight_t, turn_cos, turn_sin,
+    first_wave, rest, order_near, early, line, sems, *, spans, nside
 ):
+    rows = early.shape[1]
+    early_a = pltpu.make_async_copy(a_hbm.at[:rows, :], early.at[0], sems.at[3])
+    early_b = pltpu.make_async_copy(b_hbm.at[:rows, :], early.at[1], sems.at[4])
     cos_phi = pltpu.make_async_copy(table_hbm.at[spans["cos_phi"], :], turn_cos, sems.at[0])
     sin_phi = pltpu.make_async_copy(table_hbm.at[spans["sin_phi"], :], turn_sin, sems.at[1])
     other = pltpu.make_async_copy(table_hbm.at[spans["rest"], :], rest, sems.at[2])
     cos_phi.start()
     sin_phi.start()
     other.start()
+    early_a.start()
+    early_b.start()
     col_t[...] = jnp.transpose(col[...])
     weight_t[...] = jnp.transpose(weight[...])
     order_near[...] = order[...]
@@ -113,9 +129,11 @@
     turn_cos[...] = base_cos * shift_cos + base_sin * shift_sin
     turn_sin[...] = base_sin * shift_cos - base_cos * shift_sin
     other.wait()
-
-
-def cycle_geometry(cycle_ids, col, weight, order, owned, cycle_length, table, spans):
+    early_a.wait()
+    early_b.wait()
+
+
+def cycle_geometry(cycle_ids, col, weight, order, owned, cycle_length, table, spans, flat_a, flat_b):
     vmem = pl.BlockSpec(memory_space=pltpu.VMEM)
     square = (LANES, LANES)
     rest = spans["rest"].stop - spans["rest"].start
@@ -129,15 +147,16 @@
             jax.ShapeDtypeStruct((owned, LANES), jnp.int32),
             jax.ShapeDtypeStruct((rest, LANES), jnp.float32),
             jax.ShapeDtypeStruct(order.shape, jnp.int32),
+            jax.ShapeDtypeStruct(early_shape(flat_a.shape, owned), flat_a.dtype),
         ),
         in_specs=[pl.BlockSpec(memory_space=pltpu.SMEM), vmem, vmem, vmem]
-        + [pl.BlockSpec(memory_space=pltpu.HBM)],
-        out_specs=(vmem,) * 7,
-        scratch_shapes=[pltpu.VMEM(square, jnp.int32), pltpu.SemaphoreType.DMA((3,))],
+        + [pl.BlockSpec(memory_space=pltpu.HBM)] * 3,
+        out_specs=(vmem,) * 8,
+        scratch_shapes=[pltpu.VMEM(square, jnp.int32), pltpu.SemaphoreType.DMA((5,))],
         compiler_params=pltpu.CompilerParams(vmem_limit_bytes=VMEM_ALL - ROOM),
         cost_estimate=pl.CostEstimate(flops=10**7, bytes_accessed=10**7, transcendentals=0),
         name="geometry",
-    )(cycle_ids, col, weight, order, table)
+    )(cycle_ids, *[far(x) for x in (col, weight, order, table, flat_a, flat_b)])
 
 
 def modes_kernel(
@@ -235,7 +254,7 @@
 
 
 def cycle_modes(cycle_ids, received, geometry, components, cycle_length, per, paired, spans):
-    col_t, weight_t, turn_cos, turn_sin, _, rest, order = geometry
+    col_t, weight_t, turn_cos, turn_sin, _, rest, order, _ = geometry
     rows = order.shape[0]
     vmem = pl.BlockSpec(memory_space=pltpu.VMEM)
     return pl.pallas_call(
@@ -258,8 +277,8 @@
 
 
 def legendre_kernel(
-    modes, first_wave, a_hbm, b_hbm, div_hbm, vort_hbm, table_a, table_b, spread, div, vort, in_sems,
-    out_sems, *, levels, cycles, group, split
+    modes, first_wave, early, a_hbm, b_hbm, div_hbm, vort_hbm, table_a, table_b, spread, div, vort,
+    in_sems, out_sems, *, levels, cycles, group, split
 ):
     owned = spread.shape[1]
     width = group * cycles
@@ -278,7 +297,8 @@
             source.at[:, :, rows, :], target.at[:, :, rows, :], out_sems.at[g, which]
         )
 
-    for g in range(groups):
+    ready = early.shape[1] // width
+    for g in range(ready, groups):
         for which in range(2):
             fetch(g, which).start()
     rows = modes.shape[0]
@@ -312,14 +332,16 @@
                 pieces.append(jnp.concatenate([left, right], axis=1))
         mix = jnp.concatenate(pieces, axis=0)
         waves = first_wave[base : base + group, :]
-        fetch(g, 0).wait()
-        fetch(g, 1).wait()
+        if g >= ready:
+            fetch(g, 0).wait()
+            fetch(g, 1).wait()
         for start in range(0, degrees, chunk):
             at_rows = slice(g * width, (g + 1) * width)
-            both = jnp.concatenate(
-                [table_a[at_rows, start : start + chunk], table_b[at_rows, start : start + chunk]],
-                axis=0,
-            )
+            lanes = slice(start, start + chunk)
+            if g < ready:
+                both = jnp.concatenate([early[0, at_rows, lanes], early[1, at_rows, lanes]], axis=0)
+            else:
+                both = jnp.concatenate([table_a[at_rows, lanes], table_b[at_rows, lanes]], axis=0)
             result = jnp.dot(mix, both, preferred_element_type=jnp.float32)
             for at in range(0, chunk, LANES):
                 degree = lax.broadcasted_iota(jnp.int32, (group, LANES), 1) + (start + at)
@@ -339,10 +361,10 @@
         flush(g, 1).wait()
 
 
-def legendre_sums(modes, first_wave, legendre_a, legendre_b, levels, split):
-    owned, cycles, degrees = legendre_a.shape
-    group = math.gcd(owned, 16)
-    flat = (owned * cycles, degrees)
+def legendre_sums(modes, first_wave, early, flat_a, flat_b, owned, levels, split):
+    flat = flat_a.shape
+    cycles, degrees = flat[0] // owned, flat[1]
+    group = math.gcd(owned, GROUP)
     full = (2, levels, owned, degrees)
     out_shape = jax.ShapeDtypeStruct(full, jnp.float32)
     vmem = pl.BlockSpec(memory_space=pltpu.VMEM)
@@ -352,7 +374,7 @@
             legendre_kernel, levels=levels, cycles=cycles, group=group, split=split
         ),
         out_shape=(out_shape, out_shape),
-        in_specs=[vmem, vmem, hbm, hbm],
+        in_specs=[vmem, vmem, vmem, hbm, hbm],
         out_specs=(hbm, hbm),
         scratch_shapes=[
             pltpu.VMEM(flat, jnp.bfloat16),
@@ -365,7 +387,7 @@
         ],
         compiler_params=pltpu.CompilerParams(vmem_limit_bytes=VMEM_ALL - ROOM),
         name="legendre",
-    )(modes, first_wave, legendre_a.reshape(flat), legendre_b.reshape(flat))
+    )(modes, first_wave, early, far(flat_a), far(flat_b))
 
 
 def local(winds, remap_w, remap_col, block_pick, cycle_ids, wave_ids, legendre_a, legendre_b):
@@ -383,6 +405,8 @@
     outgoing = pick_blocks(block_pick, blocks, band_count, per)
     received = lax.all_to_all(outgoing, "band", split_axis=0, concat_axis=0, tiled=True)
     paired = 2 * owned == LANES
+    flat_a = legendre_a.reshape(-1, legendre_a.shape[2])
+    flat_b = legendre_b.reshape(-1, legendre_b.shape[2])
     table, spans = tables(cycle_length, taps, waves)
     order = wave_ids.reshape(waves // LANES, LANES)
     geometry = cycle_geometry(
@@ -394,11 +418,12 @@
         cycle_length,
         jnp.asarray(table),
         spans,
+        flat_a,
+        flat_b,
     )
     chosen = cycle_modes(
         cycle_ids, received, geometry, components, cycle_length, per, paired, spans
     )
-    first_wave = geometry[4]
     split = 2 if paired else 1
     if paired:
         parcels = chosen.reshape(devices, split, LANES)
@@ -408,7 +433,9 @@
         ).reshape(devices, 1, 4 * owned)
     gathered = lax.all_to_all(parcels, ("band", "lev"), split_axis=0, concat_axis=0, tiled=True)
     modes = gathered.reshape(devices * split, 4 * owned // split)
-    return legendre_sums(modes, first_wave, legendre_a, legendre_b, level_count, split)
+    return legendre_sums(
+        modes, geometry[4], geometry[7], flat_a, flat_b, owned, level_count, split
+    )
 
 
 def solution(mesh):

time: 34.7 us -> 34.4 us (level)
  local copies, waits for them, and re-layouts: 3.38 us -> 0 us
  Pallas kernels: 9.22 us -> 11.5 us
  waiting for transfers between devices: 3 us -> 4.15 us
  blocking collectives: 10.1 us -> 9.67 us
    unnamed x8 -> x0, local copies, waits for them, and re-layouts: 3.38 us -> none
    pallas_call x1, Pallas kernels: 0.4 us -> 2.65 us  [cycle_geometry(): pl.pallas_call(functools.partial(geometry_kernel, spans=spans, nside=cycl...]
    all_to_all x1, waiting for transfers between devices: 3 us -> 4.15 us  [local(): lax.all_to_all(outgoing, 'band', split_axis=0, concat_axis=0, tiled=True)]
    all_to_all x1, blocking collectives: 10.1 us -> 9.67 us  [local(): lax.all_to_all(parcels, ('band', 'lev'), split_axis=0, concat_axis=0, til...]
  transfers between devices with their start and end apart: 1 -> 1, of which waited for: 1 -> 1; matrix products, arithmetic and copies ran while one was open for 0% -> 0% of each run, Pallas kernels for 1% -> 8%
where the time goes in v2:
time: 34.4 us; the launch traced here: 34 us
  Pallas kernels  11.5 us (33%)
  blocking collectives  9.67 us (28%)
  starting transfers between devices  7.31 us (21%)
  waiting for transfers between devices  4.15 us (12%)
  between operations  1.3 us (4%)
    all_to_all x1, blocking collectives, local(): lax.all_to_all(parcels, ('band', 'lev'), split_axis=0, concat_axis=0, til...  9.67 us
    all_to_all x1, starting transfers between devices, local(): lax.all_to_all(outgoing, 'band', split_axis=0, concat_axis=0, tiled=True)  7.31 us
    pallas_call x1, Pallas kernels, legendre_sums(): pl.pallas_call(functools.partial(legendre_kernel, levels=levels, cycles=c...  5.12 us
    all_to_all x1, waiting for transfers between devices, local(): lax.all_to_all(outgoing, 'band', split_axis=0, concat_axis=0, tiled=True)  4.15 us
    pallas_call x1, Pallas kernels, cycle_geometry(): pl.pallas_call(functools.partial(geometry_kernel, spans=spans, nside=cycl...  2.65 us
    pallas_call x1, Pallas kernels, cycle_modes(): pl.pallas_call(functools.partial(modes_kernel, spans=spans, per=per, nsid...  1.93 us
    pallas_call x1, Pallas kernels, pick_blocks(): pl.pallas_call(functools.partial(pick_kernel, per=per), out_shape=jax.Sha...  1.84 us
  transfers between devices with their start and end apart: 1, of which 1 were waited for; matrix products, arithmetic and copies ran while one was open for 0% of the time, Pallas kernels for 8%

profile of v2, /device:TPU:0, one launch (start us, length us, event | category | flops | bytes accessed | tf_op | source)
XLA Modules:
  0.0 34.0 jit_solution(11026295511685047713)
XLA Ops:
  0.6 1.8 %pick.1 = f32[8,9,4,128]{3,2,1,0:T(4,128)} custom-call(s32[8,96]{1,0:T(8,128)} %picks.1, f32[3,256,128]{2,1,0:T(8,128)} %bitcast.14), custom_call_target="tpu_custom_call" | custom-call | tf_op jit(solution)/shard_map/pick/pallas_call | solution.py:44
  2.5 7.3 %all-to-all-start = ((f32[8,9,4,128]{3,2,1,0:T(4,128)}), f32[8,9,4,128]{3,2,1,0:T(4,128)S(1)}, u32[]{:S(2)}, u32[]{:S(2)}) async-start(f32[8,9,4,128]{3,2,1,0:T(4,128)} %pick.1), calls=%async_computation | async-start | bytes 294912 | tf_op jit(solution)/shard_map/all_to_all | solution.py:406
  10.4 2.6 %geometry.1 = (s32[128,128]{1,0:T(8,128)S(1)}, f32[128,128]{1,0:T(8,128)S(1)}, f32[128,128]{1,0:T(8,128)S(1)}, f32[128,128]{1,0:T(8,128)S(1)}, s32[64,128]{1,0:T...) custom-call(s32[1]{0:T(128)S(6)} %copy.11.cycle, ...), custom_call_target="tpu_custom_call" | custom-call | flops 10000000 | bytes 10000000 | tf_op jit(solution)/shard_map/geometry/pallas_call | solution.py:140
  13.1 4.1 %all-to-all-done.received = f32[8,9,4,128]{3,2,1,0:T(4,128)S(1)} async-done(((f32[8,9,4,128]{3,2,1,0:T(4,128)}), f32[8,9,4,128]{3,2,1,0:T(4,128)S(1)}, u32[]{:S(2)}, u32[]{:S(2)}) %all-to-all-start) | async-done | bytes 147488 | tf_op jit(solution)/shard_map/all_to_all | solution.py:406
  17.2 1.9 %modes.1 = f32[16,4,128]{2,1,0:T(4,128)S(1)} custom-call(s32[1]{0:T(128)S(6)} %copy.11.cycle, f32[8,9,4,128]{3,2,1,0:T(4,128)S(1)} %all-to-all-done.received, s32[128,128]{1,0:T(8,128)S(1)} %get-tuple-element.10.col_t, f32[128,128]{1,0:T(8,128)S(1)} %get-tuple-element.11.weight_t, f32[128,128]{1,0:T(8,128)S(1)} %get-tuple-element.12.turn_cos, ...), custom_call_target="tpu_custom_call" | custom-call | tf_op jit(solution)/shard_map/modes/pallas_call | solution.py:260
  19.2 9.7 %all_to_all.10 = f32[32,2,128]{2,1,0:T(2,128)S(1)} all-to-all(f32[32,2,128]{2,1,0:T(2,128)S(1)} %bitcast.9), channel_id=1, replica_groups=mesh['band'=8,'lev'=4] {'band','lev'}, dimensions={0} | all-to-all | bytes 65536 | tf_op jit(solution)/shard_map/all_to_all | solution.py:434
  28.8 5.1 %legendre.1 = (f32[2,4,64,2048]{3,2,1,0:T(8,128)}, f32[2,4,64,2048]{3,2,1,0:T(8,128)}) custom-call(f32[64,128]{1,0:T(8,128)S(1)} %bitcast.8, s32[64,128]{1,0:T(8,128)S(1)} %get-tuple-element.16.first_wave, bf16[2,256,2048]{2,1,0:T(8,128)(2,1)S(1)} %get-tuple-element.17.early, bf16[512,2048]{1,0:T(8,128)(2,1)} %bitcast.11, bf16[512,2048]{1,0:T(8,128)(2,1)} %bitcast.13), custom_call_target="tpu_custom_call" | custom-call | tf_op jit(solution)/shard_map/legendre/pallas_call | solution.py:372
Async XLA Ops:
  2.5 14.8 %all-to-all-start = ((f32[8,9,4,128]{3,2,1,0:T(4,128)}), f32[8,9,4,128]{3,2,1,0:T(4,128)S(1)}, u32[]{:S(2)}, u32[]{:S(2)}) async-start(f32[8,9,4,128]{3,2,1,0:T(4,128)} %pick.1), calls=%async_computation | async-start | bytes 294912 | tf_op jit(solution)/shard_map/all_to_all | solution.py:406

commit v3 on v2

--- a/solution.py
+++ b/solution.py
@@ -16,7 +16,6 @@
 EARLY = 2
 VMEM_ALL = 67043328
 ROOM = 24000 * 1024
-HIGHEST = lax.Precision.HIGHEST
 
 
 def far(array):
@@ -91,26 +90,42 @@
     return np.concatenate(list(parts.values()), 0).astype(np.float32), spans
 
 
+def placement(cycles, kinds, group):
+    row = np.arange(cycles * kinds)[:, None]
+    lane = np.arange(kinds * group * cycles)[None, :]
+    same = (row % kinds == lane // (group * cycles)) & (row // kinds == lane % cycles)
+    return jnp.asarray(same, jnp.bfloat16)
+
+
 def early_shape(flat, owned):
     group = math.gcd(owned, GROUP)
     return (2, min(EARLY, owned // group) * group * (flat[0] // owned), flat[1])
 
 
 def geometry_kernel(
-    cycle, col, weight, order, table_hbm, a_hbm, b_hbm, col_t, weight_t, turn_cos, turn_sin,
-    first_wave, rest, order_near, early, line, sems, *, spans, nside
+    cycle, col, weight, order, table_hbm, a_hbm, b_hbm, place_hbm, col_t, weight_t, turn_cos, turn_sin,
+    first_wave, rest, order_near, early, place, line, sems, *, spans, nside
 ):
     rows = early.shape[1]
-    early_a = pltpu.make_async_copy(a_hbm.at[:rows, :], early.at[0], sems.at[3])
-    early_b = pltpu.make_async_copy(b_hbm.at[:rows, :], early.at[1], sems.at[4])
+    pieces = 4
+    step = rows // pieces
+    bulk = [pltpu.make_async_copy(place_hbm, place, sems.at[3])] + [
+        pltpu.make_async_copy(
+            source.at[pl.ds(i * step, step), :],
+            early.at[which, pl.ds(i * step, step), :],
+            sems.at[4 + which * pieces + i],
+        )
+        for i in range(pieces)
+        for which, source in enumerate((a_hbm, b_hbm))
+    ]
     cos_phi = pltpu.make_async_copy(table_hbm.at[spans["cos_phi"], :], turn_cos, sems.at[0])
     sin_phi = pltpu.make_async_copy(table_hbm.at[spans["sin_phi"], :], turn_sin, sems.at[1])
     other = pltpu.make_async_copy(table_hbm.at[spans["rest"], :], rest, sems.at[2])
     cos_phi.start()
     sin_phi.start()
     other.start()
-    early_a.start()
-    early_b.start()
+    for copy in bulk:
+        copy.start()
     col_t[...] = jnp.transpose(col[...])
     weight_t[...] = jnp.transpose(weight[...])
     order_near[...] = order[...]
@@ -129,16 +144,22 @@
     turn_cos[...] = base_cos * shift_cos + base_sin * shift_sin
     turn_sin[...] = base_sin * shift_cos - base_cos * shift_sin
     other.wait()
-    early_a.wait()
-    early_b.wait()
-
-
-def cycle_geometry(cycle_ids, col, weight, order, owned, cycle_length, table, spans, flat_a, flat_b):
+    for copy in bulk:
+        copy.wait()
+
+
+def cycle_geometry(
+    cycle_ids, col, weight, order, owned, levels, split, cycle_length, table, spans, flat_a, flat_b
+):
+    cycles = flat_a.shape[0] // owned
+    place = placement(cycles, levels * split, math.gcd(owned, GROUP))
     vmem = pl.BlockSpec(memory_space=pltpu.VMEM)
     square = (LANES, LANES)
     rest = spans["rest"].stop - spans["rest"].start
     return pl.pallas_call(
-        functools.partial(geometry_kernel, spans=spans, nside=cycle_length // 4),
+        functools.partial(
+            geometry_kernel, spans=spans, nside=cycle_length // 4
+        ),
         out_shape=(
             jax.ShapeDtypeStruct(square, jnp.int32),
             jax.ShapeDtypeStruct(square, jnp.float32),
@@ -148,15 +169,25 @@
             jax.ShapeDtypeStruct((rest, LANES), jnp.float32),
             jax.ShapeDtypeStruct(order.shape, jnp.int32),
             jax.ShapeDtypeStruct(early_shape(flat_a.shape, owned), flat_a.dtype),
+            jax.ShapeDtypeStruct(place.shape, place.dtype),
         ),
         in_specs=[pl.BlockSpec(memory_space=pltpu.SMEM), vmem, vmem, vmem]
-        + [pl.BlockSpec(memory_space=pltpu.HBM)] * 3,
-        out_specs=(vmem,) * 8,
-        scratch_shapes=[pltpu.VMEM(square, jnp.int32), pltpu.SemaphoreType.DMA((5,))],
+        + [pl.BlockSpec(memory_space=pltpu.HBM)] * 4,
+        out_specs=(vmem,) * 9,
+        scratch_shapes=[pltpu.VMEM(square, jnp.int32), pltpu.SemaphoreType.DMA((12,))],
         compiler_params=pltpu.CompilerParams(vmem_limit_bytes=VMEM_ALL - ROOM),
         cost_estimate=pl.CostEstimate(flops=10**7, bytes_accessed=10**7, transcendentals=0),
         name="geometry",
-    )(cycle_ids, *[far(x) for x in (col, weight, order, table, flat_a, flat_b)])
+    )(cycle_ids, *[far(x) for x in (col, weight, order, table, flat_a, flat_b, place)])
+
+
+def halves(value):
+    high = value.astype(jnp.bfloat16)
+    return high, (value - high.astype(jnp.float32)).astype(jnp.bfloat16)
+
+
+def product(left, right):
+    return jnp.dot(left, right, preferred_element_type=jnp.float32)
 
 
 def modes_kernel(
@@ -172,24 +203,27 @@
     def part(name):
         return table[spans[name].start - first : spans[name].stop - first, :]
 
-    for comp in range(components):
-        for group in range(groups):
-            block_rows = [
+    for group in range(groups):
+        block_rows = [
+            [
                 received[(slice(group * SUB, (group + 1) * SUB), *divmod(comp * per + blk, quad))]
                 for blk in range(per)
             ]
-            for tile in range(group, tiles, groups):
-                index = col_t[tile * SUB : (tile + 1) * SUB, :]
-                lane = index & (BLK - 1)
-                block = index >> (BLK.bit_length() - 1)
-                value = jnp.take_along_axis(block_rows[0], lane, axis=1)
-                for blk in range(1, per):
-                    value = jnp.where(
-                        block == blk, jnp.take_along_axis(block_rows[blk], lane, axis=1), value
-                    )
-                cart[comp, tile * SUB : (tile + 1) * SUB, :] = (
-                    value * weight_t[tile * SUB : (tile + 1) * SUB, :]
-                )
+            for comp in range(components)
+        ]
+        for tile in range(group, tiles, groups):
+            rows = slice(tile * SUB, (tile + 1) * SUB)
+            index = col_t[rows, :]
+            lane = index & (BLK - 1)
+            block = index >> (BLK.bit_length() - 1)
+            values = [jnp.take_along_axis(part_rows[0], lane, axis=1) for part_rows in block_rows]
+            for blk in range(1, per):
+                here = block == blk
+                for comp in range(components):
+                    found = jnp.take_along_axis(block_rows[comp][blk], lane, axis=1)
+                    values[comp] = jnp.where(here, found, values[comp])
+            for comp in range(components):
+                cart[comp, rows, :] = values[comp] * weight_t[rows, :]
     number = cycle[0]
     half = lax.rem(number - nside + 1, 2) != 0
     number_f = jnp.full((SUB, LANES), number, jnp.int32).astype(jnp.float32)
@@ -203,7 +237,12 @@
     north = sin_theta * z - cos_theta * (cos_phi * x + sin_phi * y)
     samples = jnp.concatenate([east, north], axis=0)
     outer = jnp.concatenate([part("outer_real"), part("outer_imag")], axis=1)
-    section = jnp.dot(samples, outer, precision=HIGHEST, preferred_element_type=jnp.float32)
+    outer_high, outer_low = halves(outer)
+    high, low = halves(samples)
+    section = product(
+        jnp.concatenate([high, low, high], axis=1),
+        jnp.concatenate([outer_high, outer_high, outer_low], axis=0),
+    )
     twist_cos, twist_sin = part("twist_cos"), part("twist_sin")
     turned_real = []
     turned_imag = []
@@ -216,8 +255,11 @@
         [jnp.concatenate(turned_real, axis=1), jnp.concatenate(turned_imag, axis=1)], axis=0
     )
     inner = jnp.concatenate([part("inner_real"), part("inner_imag")], axis=1)
-    spectrum = jnp.dot(inner, turned, precision=HIGHEST, preferred_element_type=jnp.float32)
     rows = field.shape[1]
+    inner_high, inner_low = halves(inner)
+    high, low = halves(turned)
+    both = product(jnp.concatenate([inner_high, inner_low], axis=0), high)
+    spectrum = both[: 2 * rows] + both[2 * rows :] + product(inner_high, low)
     half_cos, half_sin = part("half_cos"), part("half_sin")
     rot_cos = jnp.where(half, half_cos, half_cos * half_cos - half_sin * half_sin)
     rot_sin = jnp.where(half, half_sin, 2.0 * half_cos * half_sin)
@@ -226,7 +268,7 @@
         imag = spectrum[rows:, f * LANES : (f + 1) * LANES]
         field[2 * f] = real * rot_cos + imag * rot_sin
         field[2 * f + 1] = imag * rot_cos - real * rot_sin
-    low = lax.broadcasted_iota(jnp.int32, (SUB, LANES), 1) < LANES // 2
+    front = lax.broadcasted_iota(jnp.int32, (SUB, LANES), 1) < LANES // 2
     for top in range(0, rows, SUB):
         wave = order[top : top + SUB, :]
         lane = wave & (LANES - 1)
@@ -243,10 +285,10 @@
             for h in range(2):
                 first_f, second_f = picked[2 * h], picked[2 * h + 1]
                 out[top : top + SUB, h, :] = jnp.where(
-                    low, first_f, pltpu.roll(second_f, LANES // 2, axis=1)
+                    front, first_f, pltpu.roll(second_f, LANES // 2, axis=1)
                 )
                 out[top : top + SUB, 2 + h, :] = jnp.where(
-                    low, pltpu.roll(first_f, LANES // 2, axis=1), second_f
+                    front, pltpu.roll(first_f, LANES // 2, axis=1), second_f
                 )
         else:
             for k in range(4):
@@ -254,7 +296,7 @@
 
 
 def cycle_modes(cycle_ids, received, geometry, components, cycle_length, per, paired, spans):
-    col_t, weight_t, turn_cos, turn_sin, _, rest, order, _ = geometry
+    col_t, weight_t, turn_cos, turn_sin, _, rest, order, _, _ = geometry
     rows = order.shape[0]
     vmem = pl.BlockSpec(memory_space=pltpu.VMEM)
     return pl.pallas_call(
@@ -277,10 +319,10 @@
 
 
 def legendre_kernel(
-    modes, first_wave, early, a_hbm, b_hbm, div_hbm, vort_hbm, table_a, table_b, spread, div, vort,
+    modes, first_wave, early, place, a_hbm, b_hbm, div_hbm, vort_hbm, table_a, table_b, turned, div, vort,
     in_sems, out_sems, *, levels, cycles, group, split
 ):
-    owned = spread.shape[1]
+    owned = turned.shape[0] * split // 4
     width = group * cycles
     groups = owned // group
     degrees = table_a.shape[1]
@@ -301,36 +343,35 @@
     for g in range(ready, groups):
         for which in range(2):
             fetch(g, which).start()
-    rows = modes.shape[0]
-    row = lax.broadcasted_iota(jnp.int32, (rows, levels * split * width), 0)
-    lane = lax.broadcasted_iota(jnp.int32, (rows, levels * split * width), 1)
-    same = (lax.rem(row, levels * split) == lax.div(lane, width)) & (
-        lax.div(row, levels * split) == lax.rem(lane, cycles)
-    )
-    pick = jnp.where(same, 1.0, 0.0).astype(jnp.bfloat16)
-    turned = jnp.transpose(modes[...]).astype(jnp.bfloat16)
-    wide = jnp.dot(turned, pick, preferred_element_type=jnp.float32)
-    slot = lax.broadcasted_iota(jnp.int32, (owned, width), 0)
-    place = lax.broadcasted_iota(jnp.int32, (owned, width), 1)
-    own = lax.rem(slot, group) == lax.div(place, cycles)
-    for f in range(4):
-        h, i = divmod(f, 4 // split)
-        for lev in range(levels):
-            start = (lev * split + h) * width
-            part = wide[i * owned : (i + 1) * owned, start : start + width]
-            spread[f * levels + lev] = jnp.where(own, part, 0.0).astype(jnp.bfloat16)
+    turned[...] = jnp.transpose(modes[...])
+    slot = lax.broadcasted_iota(jnp.int32, (group, width), 0)
+    entry = lax.broadcasted_iota(jnp.int32, (group, width), 1)
+    own = slot == lax.div(entry, cycles)
+    fields = 4 // split
     chunk = min(256, degrees)
     for g in range(groups):
         base = g * group
-        pieces = []
-        for sign_a, field_a, sign_b, field_b in PARTS:
-            for lev in range(levels):
-                left = spread[field_a * levels + lev, base : base + group, :]
-                right = spread[field_b * levels + lev, base : base + group, :]
-                left = left if sign_a > 0 else -left
-                right = right if sign_b > 0 else -right
-                pieces.append(jnp.concatenate([left, right], axis=1))
-        mix = jnp.concatenate(pieces, axis=0)
+        mine = jnp.concatenate(
+            [turned[i * owned + base : i * owned + base + group, :] for i in range(fields)], axis=0
+        ).astype(jnp.bfloat16)
+        wide = jnp.dot(mine, place[...], preferred_element_type=jnp.float32)
+
+        def spread(f, lev, sign):
+            h, i = divmod(f, fields)
+            start = (lev * split + h) * width
+            part = wide[i * group : (i + 1) * group, start : start + width]
+            return jnp.where(own, part if sign > 0 else -part, 0.0)
+
+        mix = jnp.concatenate(
+            [
+                jnp.concatenate(
+                    [spread(field_a, lev, sign_a), spread(field_b, lev, sign_b)], axis=1
+                )
+                for sign_a, field_a, sign_b, field_b in PARTS
+                for lev in range(levels)
+            ],
+            axis=0,
+        ).astype(jnp.bfloat16)
         waves = first_wave[base : base + group, :]
         if g >= ready:
             fetch(g, 0).wait()
@@ -361,7 +402,7 @@
         flush(g, 1).wait()
 
 
-def legendre_sums(modes, first_wave, early, flat_a, flat_b, owned, levels, split):
+def legendre_sums(modes, first_wave, early, place, flat_a, flat_b, owned, levels, split):
     flat = flat_a.shape
     cycles, degrees = flat[0] // owned, flat[1]
     group = math.gcd(owned, GROUP)
@@ -374,12 +415,12 @@
             legendre_kernel, levels=levels, cycles=cycles, group=group, split=split
         ),
         out_shape=(out_shape, out_shape),
-        in_specs=[vmem, vmem, vmem, hbm, hbm],
+        in_specs=[vmem, vmem, vmem, vmem, hbm, hbm],
         out_specs=(hbm, hbm),
         scratch_shapes=[
             pltpu.VMEM(flat, jnp.bfloat16),
             pltpu.VMEM(flat, jnp.bfloat16),
-            pltpu.VMEM((4 * levels, owned, group * cycles), jnp.bfloat16),
+            pltpu.VMEM(modes.shape[::-1], jnp.float32),
             pltpu.VMEM(full, jnp.float32),
             pltpu.VMEM(full, jnp.float32),
             pltpu.SemaphoreType.DMA((owned // group, 2)),
@@ -387,7 +428,7 @@
         ],
         compiler_params=pltpu.CompilerParams(vmem_limit_bytes=VMEM_ALL - ROOM),
         name="legendre",
-    )(modes, first_wave, early, far(flat_a), far(flat_b))
+    )(modes, first_wave, early, place, far(flat_a), far(flat_b))
 
 
 def local(winds, remap_w, remap_col, block_pick, cycle_ids, wave_ids, legendre_a, legendre_b):
@@ -405,6 +446,7 @@
     outgoing = pick_blocks(block_pick, blocks, band_count, per)
     received = lax.all_to_all(outgoing, "band", split_axis=0, concat_axis=0, tiled=True)
     paired = 2 * owned == LANES
+    split = 2 if paired else 1
     flat_a = legendre_a.reshape(-1, legendre_a.shape[2])
     flat_b = legendre_b.reshape(-1, legendre_b.shape[2])
     table, spans = tables(cycle_length, taps, waves)
@@ -415,6 +457,8 @@
         remap_w.reshape(LANES, LANES),
         order,
         owned,
+        level_count,
+        split,
         cycle_length,
         jnp.asarray(table),
         spans,
@@ -424,7 +468,6 @@
     chosen = cycle_modes(
         cycle_ids, received, geometry, components, cycle_length, per, paired, spans
     )
-    split = 2 if paired else 1
     if paired:
         parcels = chosen.reshape(devices, split, LANES)
     else:
@@ -434,7 +477,7 @@
     gathered = lax.all_to_all(parcels, ("band", "lev"), split_axis=0, concat_axis=0, tiled=True)
     modes = gathered.reshape(devices * split, 4 * owned // split)
     return legendre_sums(
-        modes, geometry[4], geometry[7], flat_a, flat_b, owned, level_count, split
+        modes, geometry[4], geometry[7], geometry[8], flat_a, flat_b, owned, level_count, split
     )
 
 

time: 34.4 us -> 32.8 us (0.953)
  Pallas kernels: 11.5 us -> 10.1 us
    pallas_call x1, Pallas kernels: 5.12 us -> 4.02 us  [legendre_sums(): pl.pallas_call(functools.partial(legendre_kernel, levels=levels, cycles=c...]
    pallas_call x1, Pallas kernels: 1.93 us -> 1.48 us  [cycle_modes(): pl.pallas_call(functools.partial(modes_kernel, spans=spans, per=per, nsid...]
where the time goes in v3:
time: 32.8 us; the launch traced here: 32.4 us
  Pallas kernels  10.1 us (31%)
  blocking collectives  9.67 us (29%)
  starting transfers between devices  7.31 us (22%)
  waiting for transfers between devices  4.06 us (12%)
  between operations  1.3 us (4%)
    all_to_all x1, blocking collectives, local(): lax.all_to_all(parcels, ('band', 'lev'), split_axis=0, concat_axis=0, til...  9.67 us
    all_to_all x1, starting transfers between devices, local(): lax.all_to_all(outgoing, 'band', split_axis=0, concat_axis=0, tiled=True)  7.31 us
    all_to_all x1, waiting for transfers between devices, local(): lax.all_to_all(outgoing, 'band', split_axis=0, concat_axis=0, tiled=True)  4.06 us
    pallas_call x1, Pallas kernels, legendre_sums(): pl.pallas_call(functools.partial(legendre_kernel, levels=levels, cycles=c...  4.02 us
    pallas_call x1, Pallas kernels, cycle_geometry(): pl.pallas_call(functools.partial(geometry_kernel, spans=spans, nside=cycl...  2.73 us
    pallas_call x1, Pallas kernels, pick_blocks(): pl.pallas_call(functools.partial(pick_kernel, per=per), out_shape=jax.Sha...  1.84 us
    pallas_call x1, Pallas kernels, cycle_modes(): pl.pallas_call(functools.partial(modes_kernel, spans=spans, per=per, nsid...  1.48 us
  transfers between devices with their start and end apart: 1, of which 1 were waited for; matrix products, arithmetic and copies ran while one was open for 0% of the time, Pallas kernels for 8%

profile of v3, /device:TPU:0, one launch (start us, length us, event | category | flops | bytes accessed | tf_op | source)
XLA Modules:
  0.0 32.4 jit_solution(14967187536835492099)
XLA Ops:
  0.6 1.8 %pick.1 = f32[8,9,4,128]{3,2,1,0:T(4,128)} custom-call(s32[8,96]{1,0:T(8,128)} %picks.1, f32[3,256,128]{2,1,0:T(8,128)} %bitcast.14), custom_call_target="tpu_custom_call" | custom-call | tf_op jit(solution)/shard_map/pick/pallas_call | solution.py:43
  2.5 7.3 %all-to-all-start = ((f32[8,9,4,128]{3,2,1,0:T(4,128)}), f32[8,9,4,128]{3,2,1,0:T(4,128)S(1)}, u32[]{:S(2)}, u32[]{:S(2)}) async-start(f32[8,9,4,128]{3,2,1,0:T(4,128)} %pick.1), calls=%async_computation | async-start | bytes 294912 | tf_op jit(solution)/shard_map/all_to_all | solution.py:447
  10.4 2.7 %geometry.1 = (s32[128,128]{1,0:T(8,128)S(1)}, f32[128,128]{1,0:T(8,128)S(1)}, f32[128,128]{1,0:T(8,128)S(1)}, f32[128,128]{1,0:T(8,128)S(1)}, s32[64,128]{1,0:T...) custom-call(s32[1]{0:T(128)S(6)} %copy.12.cycle, ...), custom_call_target="tpu_custom_call" | custom-call | flops 10000000 | bytes 10000000 | tf_op jit(solution)/shard_map/geometry/pallas_call | solution.py:159
  13.2 4.1 %all-to-all-done.received = f32[8,9,4,128]{3,2,1,0:T(4,128)S(1)} async-done(((f32[8,9,4,128]{3,2,1,0:T(4,128)}), f32[8,9,4,128]{3,2,1,0:T(4,128)S(1)}, u32[]{:S(2)}, u32[]{:S(2)}) %all-to-all-start) | async-done | bytes 147488 | tf_op jit(solution)/shard_map/all_to_all | solution.py:447
  17.2 1.5 %modes.1 = f32[16,4,128]{2,1,0:T(4,128)S(1)} custom-call(s32[1]{0:T(128)S(6)} %copy.12.cycle, f32[8,9,4,128]{3,2,1,0:T(4,128)S(1)} %all-to-all-done.received, s32[128,128]{1,0:T(8,128)S(1)} %get-tuple-element.11.col_t, f32[128,128]{1,0:T(8,128)S(1)} %get-tuple-element.12.weight_t, f32[128,128]{1,0:T(8,128)S(1)} %get-tuple-element.13.turn_cos, ...), custom_call_target="tpu_custom_call" | custom-call | tf_op jit(solution)/shard_map/modes/pallas_call | solution.py:302
  18.7 9.7 %all_to_all.10 = f32[32,2,128]{2,1,0:T(2,128)S(1)} all-to-all(f32[32,2,128]{2,1,0:T(2,128)S(1)} %bitcast.9), channel_id=1, replica_groups=mesh['band'=8,'lev'=4] {'band','lev'}, dimensions={0} | all-to-all | bytes 65536 | tf_op jit(solution)/shard_map/all_to_all | solution.py:477
  28.4 4.0 %legendre.1 = (f32[2,4,64,2048]{3,2,1,0:T(8,128)}, f32[2,4,64,2048]{3,2,1,0:T(8,128)}) custom-call(f32[64,128]{1,0:T(8,128)S(1)} %bitcast.8, s32[64,128]{1,0:T(8,128)S(1)} %get-tuple-element.17.first_wave, bf16[2,256,2048]{2,1,0:T(8,128)(2,1)S(1)} %get-tuple-element.18.early, bf16[64,1024]{1,0:T(8,128)(2,1)S(1)} %get-tuple-element.19.place, ...), custom_call_target="tpu_custom_call" | custom-call | tf_op jit(solution)/shard_map/legendre/pallas_call | solution.py:413
Async XLA Ops:
  2.5 14.8 %all-to-all-start = ((f32[8,9,4,128]{3,2,1,0:T(4,128)}), f32[8,9,4,128]{3,2,1,0:T(4,128)S(1)}, u32[]{:S(2)}, u32[]{:S(2)}) async-start(f32[8,9,4,128]{3,2,1,0:T(4,128)} %pick.1), calls=%async_computation | async-start | bytes 294912 | tf_op jit(solution)/shard_map/all_to_all | solution.py:447

commit v4 on v3

--- a/solution.py
+++ b/solution.py
@@ -194,8 +194,9 @@
     cycle, received, col_t, weight_t, turn_cos, turn_sin, order, table, out, cart, field,
     *, spans, per, nside, paired
 ):
-    band_count, _, quad, _ = received.shape
     components = cart.shape[0]
+    span = components * per
+    band_count = received.shape[0] // span
     tiles = LANES // SUB
     groups = band_count // SUB
     first = spans["rest"].start
@@ -206,7 +207,7 @@
     for group in range(groups):
         block_rows = [
             [
-                received[(slice(group * SUB, (group + 1) * SUB), *divmod(comp * per + blk, quad))]
+                received[pl.ds(group * SUB * span + comp * per + blk, SUB, stride=span), :]
                 for blk in range(per)
             ]
             for comp in range(components)
@@ -445,6 +446,7 @@
     blocks = winds.reshape(components, column_count // BLK, BLK)
     outgoing = pick_blocks(block_pick, blocks, band_count, per)
     received = lax.all_to_all(outgoing, "band", split_axis=0, concat_axis=0, tiled=True)
+    received = received.reshape(band_count * components * per, BLK)
     paired = 2 * owned == LANES
     split = 2 if paired else 1
     flat_a = legendre_a.reshape(-1, legendre_a.shape[2])
@@ -472,7 +474,7 @@
         parcels = chosen.reshape(devices, split, LANES)
     else:
         parcels = jnp.transpose(
-            jnp.transpose(chosen, (1, 0, 2)).reshape(4, devices, owned), (1, 0, 2)
+            jnp.transpose(chosen.reshape(-1, 4, LANES), (1, 0, 2)).reshape(4, devices, owned), (1, 0, 2)
         ).reshape(devices, 1, 4 * owned)
     gathered = lax.all_to_all(parcels, ("band", "lev"), split_axis=0, concat_axis=0, tiled=True)
     modes = gathered.reshape(devices * split, 4 * owned // split)

time: 32.8 us -> 32.8 us (level)
  no operation moved by 1% of the time
where the time goes in v4:
time: 32.8 us; the launch traced here: 32.4 us
  Pallas kernels  10 us (30%)
  blocking collectives  9.68 us (30%)
  starting transfers between devices  7.31 us (22%)
  waiting for transfers between devices  4.06 us (12%)
  between operations  1.3 us (4%)
    all_to_all x1, blocking collectives, local(): lax.all_to_all(parcels, ('band', 'lev'), split_axis=0, concat_axis=0, til...  9.68 us
    all_to_all x1, starting transfers between devices, local(): lax.all_to_all(outgoing, 'band', split_axis=0, concat_axis=0, tiled=True)  7.31 us
    all_to_all x1, waiting for transfers between devices, local(): lax.all_to_all(outgoing, 'band', split_axis=0, concat_axis=0, tiled=True)  4.06 us
    pallas_call x1, Pallas kernels, legendre_sums(): pl.pallas_call(functools.partial(legendre_kernel, levels=levels, cycles=c...  4.02 us
    pallas_call x1, Pallas kernels, cycle_geometry(): pl.pallas_call(functools.partial(geometry_kernel, spans=spans, nside=cycl...  2.73 us
    pallas_call x1, Pallas kernels, pick_blocks(): pl.pallas_call(functools.partial(pick_kernel, per=per), out_shape=jax.Sha...  1.84 us
    pallas_call x1, Pallas kernels, cycle_modes(): pl.pallas_call(functools.partial(modes_kernel, spans=spans, per=per, nsid...  1.44 us
  transfers between devices with their start and end apart: 1, of which 1 were waited for; matrix products, arithmetic and copies ran while one was open for 0% of the time, Pallas kernels for 8%

profile of v4, /device:TPU:0, one launch (start us, length us, event | category | flops | bytes accessed | tf_op | source)
XLA Modules:
  0.0 32.4 jit_solution(1603716171772298738)
XLA Ops:
  0.6 1.8 %pick.1 = f32[8,9,4,128]{3,2,1,0:T(4,128)} custom-call(s32[8,96]{1,0:T(8,128)} %picks.1, f32[3,256,128]{2,1,0:T(8,128)} %bitcast.16), custom_call_target="tpu_custom_call" | custom-call | tf_op jit(solution)/shard_map/pick/pallas_call | solution.py:43
  2.5 7.3 %all-to-all-start = ((f32[8,9,4,128]{3,2,1,0:T(4,128)}), f32[8,9,4,128]{3,2,1,0:T(4,128)S(1)}, u32[]{:S(2)}, u32[]{:S(2)}) async-start(f32[8,9,4,128]{3,2,1,0:T(4,128)} %pick.1), calls=%async_computation | async-start | bytes 294912 | tf_op jit(solution)/shard_map/all_to_all | solution.py:448
  10.4 2.7 %geometry.1 = (s32[128,128]{1,0:T(8,128)S(1)}, f32[128,128]{1,0:T(8,128)S(1)}, f32[128,128]{1,0:T(8,128)S(1)}, f32[128,128]{1,0:T(8,128)S(1)}, s32[64,128]{1,0:T...) custom-call(s32[1]{0:T(128)S(6)} %copy.12.cycle, ...), custom_call_target="tpu_custom_call" | custom-call | flops 10000000 | bytes 10000000 | tf_op jit(solution)/shard_map/geometry/pallas_call | solution.py:159
  13.2 4.1 %all-to-all-done = f32[8,9,4,128]{3,2,1,0:T(4,128)S(1)} async-done(((f32[8,9,4,128]{3,2,1,0:T(4,128)}), f32[8,9,4,128]{3,2,1,0:T(4,128)S(1)}, u32[]{:S(2)}, u32[]{:S(2)}) %all-to-all-start) | async-done | bytes 147488 | tf_op jit(solution)/shard_map/all_to_all | solution.py:448
  17.2 1.4 %modes.1 = f32[16,4,128]{2,1,0:T(4,128)S(1)} custom-call(s32[1]{0:T(128)S(6)} %copy.12.cycle, f32[288,128]{1,0:T(8,128)S(1)} %bitcast.9, s32[128,128]{1,0:T(8,128)S(1)} %get-tuple-element.11.col_t, f32[128,128]{1,0:T(8,128)S(1)} %get-tuple-element.12.weight_t, f32[128,128]{1,0:T(8,128)S(1)} %get-tuple-element.13.turn_cos, ...), custom_call_target="tpu_custom_call" | custom-call | tf_op jit(solution)/shard_map/modes/pallas_call | solution.py:303
  18.7 9.7 %all_to_all.10 = f32[32,2,128]{2,1,0:T(2,128)S(1)} all-to-all(f32[32,2,128]{2,1,0:T(2,128)S(1)} %bitcast.11), channel_id=1, replica_groups=mesh['band'=8,'lev'=4] {'band','lev'}, dimensions={0} | all-to-all | bytes 65536 | tf_op jit(solution)/shard_map/all_to_all | solution.py:479
  28.4 4.0 %legendre.1 = (f32[2,4,64,2048]{3,2,1,0:T(8,128)}, f32[2,4,64,2048]{3,2,1,0:T(8,128)}) custom-call(f32[64,128]{1,0:T(8,128)S(1)} %bitcast.10, s32[64,128]{1,0:T(8,128)S(1)} %get-tuple-element.17.first_wave, bf16[2,256,2048]{2,1,0:T(8,128)(2,1)S(1)} %get-tuple-element.18.early, bf16[64,1024]{1,0:T(8,128)(2,1)S(1)} %get-tuple-element.19.place, ...), custom_call_target="tpu_custom_call" | custom-call | tf_op jit(solution)/shard_map/legendre/pallas_call | solution.py:414
Async XLA Ops:
  2.5 14.8 %all-to-all-start = ((f32[8,9,4,128]{3,2,1,0:T(4,128)}), f32[8,9,4,128]{3,2,1,0:T(4,128)S(1)}, u32[]{:S(2)}, u32[]{:S(2)}) async-start(f32[8,9,4,128]{3,2,1,0:T(4,128)} %pick.1), calls=%async_computation | async-start | bytes 294912 | tf_op jit(solution)/shard_map/all_to_all | solution.py:448

commit v5 on v4

--- a/solution.py
+++ b/solution.py
@@ -350,10 +350,10 @@
     own = slot == lax.div(entry, cycles)
     fields = 4 // split
     chunk = min(256, degrees)
-    for g in range(groups):
-        base = g * group
+    def one_group(g, tables_of, late):
+        base = pl.multiple_of(g * group, group)
         mine = jnp.concatenate(
-            [turned[i * owned + base : i * owned + base + group, :] for i in range(fields)], axis=0
+            [turned[pl.ds(i * owned + base, group), :] for i in range(fields)], axis=0
         ).astype(jnp.bfloat16)
         wide = jnp.dot(mine, place[...], preferred_element_type=jnp.float32)
 
@@ -373,17 +373,14 @@
             ],
             axis=0,
         ).astype(jnp.bfloat16)
-        waves = first_wave[base : base + group, :]
-        if g >= ready:
+        waves = first_wave[pl.ds(base, group), :]
+        if late:
             fetch(g, 0).wait()
             fetch(g, 1).wait()
         for start in range(0, degrees, chunk):
-            at_rows = slice(g * width, (g + 1) * width)
+            at_rows = pl.ds(pl.multiple_of(g * width, width), width)
             lanes = slice(start, start + chunk)
-            if g < ready:
-                both = jnp.concatenate([early[0, at_rows, lanes], early[1, at_rows, lanes]], axis=0)
-            else:
-                both = jnp.concatenate([table_a[at_rows, lanes], table_b[at_rows, lanes]], axis=0)
+            both = jnp.concatenate([table[at_rows, lanes] for table in tables_of], axis=0)
             result = jnp.dot(mix, both, preferred_element_type=jnp.float32)
             for at in range(0, chunk, LANES):
                 degree = lax.broadcasted_iota(jnp.int32, (group, LANES), 1) + (start + at)
@@ -393,11 +390,21 @@
                     for lev in range(levels):
                         top = (part * levels + lev) * group
                         lanes = slice(start + at, start + at + LANES)
-                        target[part % 2, lev, base : base + group, lanes] = jnp.where(
+                        target[part % 2, lev, pl.ds(base, group), lanes] = jnp.where(
                             upper, result[top : top + group, at : at + LANES], 0.0
                         )
         flush(g, 0).start()
         flush(g, 1).start()
+    def ready_group(g, carry):
+        one_group(g, (early.at[0], early.at[1]), False)
+        return carry
+
+    def late_group(g, carry):
+        one_group(g, (table_a, table_b), True)
+        return carry
+
+    lax.fori_loop(0, ready, ready_group, 0)
+    lax.fori_loop(ready, groups, late_group, 0)
     for g in range(groups):
         flush(g, 0).wait()
         flush(g, 1).wait()

time: 32.8 us -> 32.8 us (level)
  no operation moved by 1% of the time
where the time goes in v5:
time: 32.8 us; the launch traced here: 32.4 us
  Pallas kernels  10.1 us (31%)
  blocking collectives  9.68 us (30%)
  starting transfers between devices  7.31 us (22%)
  waiting for transfers between devices  4.06 us (12%)
  between operations  1.3 us (4%)
    all_to_all x1, blocking collectives, local(): lax.all_to_all(parcels, ('band', 'lev'), split_axis=0, concat_axis=0, til...  9.68 us
    all_to_all x1, starting transfers between devices, local(): lax.all_to_all(outgoing, 'band', split_axis=0, concat_axis=0, tiled=True)  7.31 us
    pallas_call x1, Pallas kernels, legendre_sums(): pl.pallas_call(functools.partial(legendre_kernel, levels=levels, cycles=c...  4.06 us
    all_to_all x1, waiting for transfers between devices, local(): lax.all_to_all(outgoing, 'band', split_axis=0, concat_axis=0, tiled=True)  4.06 us
    pallas_call x1, Pallas kernels, cycle_geometry(): pl.pallas_call(functools.partial(geometry_kernel, spans=spans, nside=cycl...  2.73 us
    pallas_call x1, Pallas kernels, pick_blocks(): pl.pallas_call(functools.partial(pick_kernel, per=per), out_shape=jax.Sha...  1.84 us
    pallas_call x1, Pallas kernels, cycle_modes(): pl.pallas_call(functools.partial(modes_kernel, spans=spans, per=per, nsid...  1.44 us
  transfers between devices with their start and end apart: 1, of which 1 were waited for; matrix products, arithmetic and copies ran while one was open for 0% of the time, Pallas kernels for 8%

profile of v5, /device:TPU:0, one launch (start us, length us, event | category | flops | bytes accessed | tf_op | source)
XLA Modules:
  0.0 32.4 jit_solution(12610290869763940203)
XLA Ops:
  0.6 1.8 %pick.1 = f32[8,9,4,128]{3,2,1,0:T(4,128)} custom-call(s32[8,96]{1,0:T(8,128)} %picks.1, f32[3,256,128]{2,1,0:T(8,128)} %bitcast.16), custom_call_target="tpu_custom_call" | custom-call | tf_op jit(solution)/shard_map/pick/pallas_call | solution.py:43
  2.5 7.3 %all-to-all-start = ((f32[8,9,4,128]{3,2,1,0:T(4,128)}), f32[8,9,4,128]{3,2,1,0:T(4,128)S(1)}, u32[]{:S(2)}, u32[]{:S(2)}) async-start(f32[8,9,4,128]{3,2,1,0:T(4,128)} %pick.1), calls=%async_computation | async-start | bytes 294912 | tf_op jit(solution)/shard_map/all_to_all | solution.py:455
  10.4 2.7 %geometry.1 = (s32[128,128]{1,0:T(8,128)S(1)}, f32[128,128]{1,0:T(8,128)S(1)}, f32[128,128]{1,0:T(8,128)S(1)}, f32[128,128]{1,0:T(8,128)S(1)}, s32[64,128]{1,0:T...) custom-call(s32[1]{0:T(128)S(6)} %copy.12.cycle, ...), custom_call_target="tpu_custom_call" | custom-call | flops 10000000 | bytes 10000000 | tf_op jit(solution)/shard_map/geometry/pallas_call | solution.py:159
  13.2 4.1 %all-to-all-done = f32[8,9,4,128]{3,2,1,0:T(4,128)S(1)} async-done(((f32[8,9,4,128]{3,2,1,0:T(4,128)}), f32[8,9,4,128]{3,2,1,0:T(4,128)S(1)}, u32[]{:S(2)}, u32[]{:S(2)}) %all-to-all-start) | async-done | bytes 147488 | tf_op jit(solution)/shard_map/all_to_all | solution.py:455
  17.2 1.4 %modes.1 = f32[16,4,128]{2,1,0:T(4,128)S(1)} custom-call(s32[1]{0:T(128)S(6)} %copy.12.cycle, f32[288,128]{1,0:T(8,128)S(1)} %bitcast.9, s32[128,128]{1,0:T(8,128)S(1)} %get-tuple-element.11.col_t, f32[128,128]{1,0:T(8,128)S(1)} %get-tuple-element.12.weight_t, f32[128,128]{1,0:T(8,128)S(1)} %get-tuple-element.13.turn_cos, ...), custom_call_target="tpu_custom_call" | custom-call | tf_op jit(solution)/shard_map/modes/pallas_call | solution.py:303
  18.7 9.7 %all_to_all.10 = f32[32,2,128]{2,1,0:T(2,128)S(1)} all-to-all(f32[32,2,128]{2,1,0:T(2,128)S(1)} %bitcast.11), channel_id=1, replica_groups=mesh['band'=8,'lev'=4] {'band','lev'}, dimensions={0} | all-to-all | bytes 65536 | tf_op jit(solution)/shard_map/all_to_all | solution.py:486
  28.4 4.1 %legendre.1 = (f32[2,4,64,2048]{3,2,1,0:T(8,128)}, f32[2,4,64,2048]{3,2,1,0:T(8,128)}) custom-call(f32[64,128]{1,0:T(8,128)S(1)} %bitcast.10, s32[64,128]{1,0:T(8,128)S(1)} %get-tuple-element.17.first_wave, bf16[2,256,2048]{2,1,0:T(8,128)(2,1)S(1)} %get-tuple-element.18.early, bf16[64,1024]{1,0:T(8,128)(2,1)S(1)} %get-tuple-element.19.place, ...), custom_call_target="tpu_custom_call" | custom-call | tf_op jit(solution)/shard_map/legendre/pallas_call | solution.py:421
Async XLA Ops:
  2.5 14.8 %all-to-all-start = ((f32[8,9,4,128]{3,2,1,0:T(4,128)}), f32[8,9,4,128]{3,2,1,0:T(4,128)S(1)}, u32[]{:S(2)}, u32[]{:S(2)}) async-start(f32[8,9,4,128]{3,2,1,0:T(4,128)} %pick.1), calls=%async_computation | async-start | bytes 294912 | tf_op jit(solution)/shard_map/all_to_all | solution.py:455

commit v6 on v4

--- a/solution.py
+++ b/solution.py
@@ -12,6 +12,7 @@
 BLK = 128
 LANES = 128
 SUB = 8
+SHARES = 2
 GROUP = 16
 EARLY = 2
 VMEM_ALL = 67043328
@@ -204,27 +205,6 @@
     def part(name):
         return table[spans[name].start - first : spans[name].stop - first, :]
 
-    for group in range(groups):
-        block_rows = [
-            [
-                received[pl.ds(group * SUB * span + comp * per + blk, SUB, stride=span), :]
-                for blk in range(per)
-            ]
-            for comp in range(components)
-        ]
-        for tile in range(group, tiles, groups):
-            rows = slice(tile * SUB, (tile + 1) * SUB)
-            index = col_t[rows, :]
-            lane = index & (BLK - 1)
-            block = index >> (BLK.bit_length() - 1)
-            values = [jnp.take_along_axis(part_rows[0], lane, axis=1) for part_rows in block_rows]
-            for blk in range(1, per):
-                here = block == blk
-                for comp in range(components):
-                    found = jnp.take_along_axis(block_rows[comp][blk], lane, axis=1)
-                    values[comp] = jnp.where(here, found, values[comp])
-            for comp in range(components):
-                cart[comp, rows, :] = values[comp] * weight_t[rows, :]
     number = cycle[0]
     half = lax.rem(number - nside + 1, 2) != 0
     number_f = jnp.full((SUB, LANES), number, jnp.int32).astype(jnp.float32)
@@ -232,28 +212,48 @@
     sin_tile = jnp.sqrt(1.0 - cos_tile * cos_tile)
     cos_theta = cos_tile[:1, :]
     sin_theta = sin_tile[:1, :]
-    cos_phi, sin_phi = turn_cos[...], turn_sin[...]
-    x, y, z = cart[0], cart[1], cart[2]
-    east = cos_phi * y - sin_phi * x
-    north = sin_theta * z - cos_theta * (cos_phi * x + sin_phi * y)
-    samples = jnp.concatenate([east, north], axis=0)
     outer = jnp.concatenate([part("outer_real"), part("outer_imag")], axis=1)
     outer_high, outer_low = halves(outer)
-    high, low = halves(samples)
-    section = product(
-        jnp.concatenate([high, low, high], axis=1),
-        jnp.concatenate([outer_high, outer_high, outer_low], axis=0),
-    )
+    outer_all = jnp.concatenate([outer_high, outer_high, outer_low], axis=0)
     twist_cos, twist_sin = part("twist_cos"), part("twist_sin")
-    turned_real = []
-    turned_imag = []
-    for f in range(2):
-        real = section[f * LANES : (f + 1) * LANES, :LANES]
-        imag = section[f * LANES : (f + 1) * LANES, LANES:]
-        turned_real.append(real * twist_cos + imag * twist_sin)
-        turned_imag.append(imag * twist_cos - real * twist_sin)
+    share = LANES // SHARES
+    turned_real = [[], []]
+    turned_imag = [[], []]
+    for first_row in range(0, LANES, share):
+        for tile in range(first_row // SUB, (first_row + share) // SUB):
+            group = tile % groups
+            rows = slice(tile * SUB, (tile + 1) * SUB)
+            index = col_t[rows, :]
+            lane = index & (BLK - 1)
+            block = index >> (BLK.bit_length() - 1)
+            values = [None] * components
+            for blk in range(per):
+                here = block == blk
+                for comp in range(components):
+                    row = group * SUB * span + comp * per + blk
+                    table_rows = received[pl.ds(row, SUB, stride=span), :]
+                    found = jnp.take_along_axis(table_rows, lane, axis=1)
+                    values[comp] = found if blk == 0 else jnp.where(here, found, values[comp])
+            for comp in range(components):
+                cart[comp, rows, :] = values[comp] * weight_t[rows, :]
+        rows = slice(first_row, first_row + share)
+        cos_phi, sin_phi = turn_cos[rows, :], turn_sin[rows, :]
+        x, y, z = cart[0, rows, :], cart[1, rows, :], cart[2, rows, :]
+        east = cos_phi * y - sin_phi * x
+        north = sin_theta * z - cos_theta * (cos_phi * x + sin_phi * y)
+        high, low = halves(jnp.concatenate([east, north], axis=0))
+        section = product(jnp.concatenate([high, low, high], axis=1), outer_all)
+        for f in range(2):
+            real = section[f * share : (f + 1) * share, :LANES]
+            imag = section[f * share : (f + 1) * share, LANES:]
+            turned_real[f].append(real * twist_cos[rows] + imag * twist_sin[rows])
+            turned_imag[f].append(imag * twist_cos[rows] - real * twist_sin[rows])
     turned = jnp.concatenate(
-        [jnp.concatenate(turned_real, axis=1), jnp.concatenate(turned_imag, axis=1)], axis=0
+        [
+            jnp.concatenate([jnp.concatenate(pieces, axis=0) for pieces in kind], axis=1)
+            for kind in (turned_real, turned_imag)
+        ],
+        axis=0,
     )
     inner = jnp.concatenate([part("inner_real"), part("inner_imag")], axis=1)
     rows = field.shape[1]

time: 32.8 us -> 32.8 us (level)
  no operation moved by 1% of the time
where the time goes in v6:
time: 32.8 us; the launch traced here: 32.4 us
  Pallas kernels  10.1 us (31%)
  blocking collectives  9.67 us (29%)
  starting transfers between devices  7.31 us (22%)
  waiting for transfers between devices  4.06 us (12%)
  between operations  1.3 us (4%)
    all_to_all x1, blocking collectives, local(): lax.all_to_all(parcels, ('band', 'lev'), split_axis=0, concat_axis=0, til...  9.67 us
    all_to_all x1, starting transfers between devices, local(): lax.all_to_all(outgoing, 'band', split_axis=0, concat_axis=0, tiled=True)  7.31 us
    all_to_all x1, waiting for transfers between devices, local(): lax.all_to_all(outgoing, 'band', split_axis=0, concat_axis=0, tiled=True)  4.06 us
    pallas_call x1, Pallas kernels, legendre_sums(): pl.pallas_call(functools.partial(legendre_kernel, levels=levels, cycles=c...  4.02 us
    pallas_call x1, Pallas kernels, cycle_geometry(): pl.pallas_call(functools.partial(geometry_kernel, spans=spans, nside=cycl...  2.73 us
    pallas_call x1, Pallas kernels, pick_blocks(): pl.pallas_call(functools.partial(pick_kernel, per=per), out_shape=jax.Sha...  1.84 us
    pallas_call x1, Pallas kernels, cycle_modes(): pl.pallas_call(functools.partial(modes_kernel, spans=spans, per=per, nsid...  1.46 us
  transfers between devices with their start and end apart: 1, of which 1 were waited for; matrix products, arithmetic and copies ran while one was open for 0% of the time, Pallas kernels for 8%

profile of v6, /device:TPU:0, one launch (start us, length us, event | category | flops | bytes accessed | tf_op | source)
XLA Modules:
  0.0 32.4 jit_solution(17161605220939987265)
XLA Ops:
  0.6 1.8 %pick.1 = f32[8,9,4,128]{3,2,1,0:T(4,128)} custom-call(s32[8,96]{1,0:T(8,128)} %picks.1, f32[3,256,128]{2,1,0:T(8,128)} %bitcast.16), custom_call_target="tpu_custom_call" | custom-call | tf_op jit(solution)/shard_map/pick/pallas_call | solution.py:44
  2.5 7.3 %all-to-all-start = ((f32[8,9,4,128]{3,2,1,0:T(4,128)}), f32[8,9,4,128]{3,2,1,0:T(4,128)S(1)}, u32[]{:S(2)}, u32[]{:S(2)}) async-start(f32[8,9,4,128]{3,2,1,0:T(4,128)} %pick.1), calls=%async_computation | async-start | bytes 294912 | tf_op jit(solution)/shard_map/all_to_all | solution.py:448
  10.4 2.7 %geometry.1 = (s32[128,128]{1,0:T(8,128)S(1)}, f32[128,128]{1,0:T(8,128)S(1)}, f32[128,128]{1,0:T(8,128)S(1)}, f32[128,128]{1,0:T(8,128)S(1)}, s32[64,128]{1,0:T...) custom-call(s32[1]{0:T(128)S(6)} %copy.12.cycle, ...), custom_call_target="tpu_custom_call" | custom-call | flops 10000000 | bytes 10000000 | tf_op jit(solution)/shard_map/geometry/pallas_call | solution.py:160
  13.2 4.1 %all-to-all-done = f32[8,9,4,128]{3,2,1,0:T(4,128)S(1)} async-done(((f32[8,9,4,128]{3,2,1,0:T(4,128)}), f32[8,9,4,128]{3,2,1,0:T(4,128)S(1)}, u32[]{:S(2)}, u32[]{:S(2)}) %all-to-all-start) | async-done | bytes 147488 | tf_op jit(solution)/shard_map/all_to_all | solution.py:448
  17.2 1.5 %modes.1 = f32[16,4,128]{2,1,0:T(4,128)S(1)} custom-call(s32[1]{0:T(128)S(6)} %copy.12.cycle, f32[288,128]{1,0:T(8,128)S(1)} %bitcast.9, s32[128,128]{1,0:T(8,128)S(1)} %get-tuple-element.11.col_t, f32[128,128]{1,0:T(8,128)S(1)} %get-tuple-element.12.weight_t, f32[128,128]{1,0:T(8,128)S(1)} %get-tuple-element.13.turn_cos, ...), custom_call_target="tpu_custom_call" | custom-call | tf_op jit(solution)/shard_map/modes/pallas_call | solution.py:303
  18.7 9.7 %all_to_all.10 = f32[32,2,128]{2,1,0:T(2,128)S(1)} all-to-all(f32[32,2,128]{2,1,0:T(2,128)S(1)} %bitcast.11), channel_id=1, replica_groups=mesh['band'=8,'lev'=4] {'band','lev'}, dimensions={0} | all-to-all | bytes 65536 | tf_op jit(solution)/shard_map/all_to_all | solution.py:479
  28.4 4.0 %legendre.1 = (f32[2,4,64,2048]{3,2,1,0:T(8,128)}, f32[2,4,64,2048]{3,2,1,0:T(8,128)}) custom-call(f32[64,128]{1,0:T(8,128)S(1)} %bitcast.10, s32[64,128]{1,0:T(8,128)S(1)} %get-tuple-element.17.first_wave, bf16[2,256,2048]{2,1,0:T(8,128)(2,1)S(1)} %get-tuple-element.18.early, bf16[64,1024]{1,0:T(8,128)(2,1)S(1)} %get-tuple-element.19.place, ...), custom_call_target="tpu_custom_call" | custom-call | tf_op jit(solution)/shard_map/legendre/pallas_call | solution.py:414
Async XLA Ops:
  2.5 14.8 %all-to-all-start = ((f32[8,9,4,128]{3,2,1,0:T(4,128)}), f32[8,9,4,128]{3,2,1,0:T(4,128)S(1)}, u32[]{:S(2)}, u32[]{:S(2)}) async-start(f32[8,9,4,128]{3,2,1,0:T(4,128)} %pick.1), calls=%async_computation | async-start | bytes 294912 | tf_op jit(solution)/shard_map/all_to_all | solution.py:448
